TPU v7x, 1024 devices: a whole 4x8x16 slice. The times are simulated.
1024 devices in a mesh: gx: 16 (over x, z_hi), gy: 8 (over y), gz: 8 (over z_lo, core).
Axes of the slice: x: 4, y: 8, z: 16 (z_hi: 4, z_lo: 4; z = z_hi * 4 + z_lo), core: 2. Of those that a mesh axis runs over, the one named last changes fastest.
Arguments:
- right_side: float32 [3, 512, 32768], P(None, None, ('gx', 'gy', 'gz')), may hold values from -6 to 6
- geometry: float32 [6, 128, 128, 1024], P(None, 'gx', 'gy', 'gz'), may hold values from -1.4 to 4, as said below
- viscosity: float32 [128, 128, 1024], P('gx', 'gy', 'gz'), may hold values from 0.3 to 3
- eig_low: float32 [1], replicated, may hold values from 0.2 to 2
- eig_high: float32 [1], replicated, may hold values from 8 to 12
- element_slot: int32 [1024, 32], P(('gx', 'gy', 'gz')), may hold values from 0 to 31, each once within a row
- dirichlet: int32 [2, 3, 128, 1024], P(None, None, 'gy', 'gz'), may hold values 0 or 1
Outputs:
- solution_field: float32 [3, 512, 32768], P(None, None, ('gx', 'gy', 'gz'))
Inputs may be any that keep to these rules, and one draw needn't show every extreme that they name: `element_slot`: each row holds each number from 0 to 31 once. `geometry`: the six entries of each node, in the order xx, yy, zz, xy, xz, yz, form a symmetric positive definite matrix.
All inputs are finite; a program needn't handle non-finite values. No bound on the sum of `dirichlet` on one device may be relied on, other than what follows from the above.
Results may differ from a plain program's by a relative error of at most 0.0003.
Values sent between devices are 32-bit elements; how exact they have to be, the bound alone decides.
A program may use at most 32 MiB of HBM per device.

v0:
```python
import jax
import jax.numpy as jnp
import numpy as np
from jax import lax
from jax.sharding import PartitionSpec as P

DEGREE = 7
ITERS = 3


helm_coefficient = 10.0


def extended_2(x, sides, width):
    for axis, dim in sides:
        size, length = (lax.axis_size(axis), x.shape[dim])
        up = [(i, (i + 1) % size) for i in range(size - 1)]
        down = [(j, i) for i, j in up]
        last = lax.slice_in_dim(x, length - width, length, axis=dim)
        first = lax.slice_in_dim(x, 0, width, axis=dim)
        before = lax.ppermute(last, axis, up)
        after = lax.ppermute(first, axis, down)
        x = jnp.concatenate([before, x, after], axis=dim)
    return x


def legendre_pair(values, degree):
    previous = 0.0 * values + 1.0
    current = values.copy()
    for order in range(2, degree + 1):
        previous, current = (
            current,
            ((2 * order - 1) * values * current - (order - 1) * previous) / order,
        )
    return (current, previous)


def gll_tables(degree):
    start = np.cos(np.pi * np.arange(degree + 1) / degree)
    nodes_now = start.copy()
    for sweep in range(80):
        top_value, lower_value = legendre_pair(nodes_now, degree)
        nodes_now = nodes_now - (nodes_now * top_value - lower_value) / ((degree + 1) * top_value)
    gll_nodes = nodes_now[::-1].copy()
    gll_nodes[0] = -1.0
    gll_nodes[degree] = 1.0
    legendre_values = legendre_pair(gll_nodes, degree)[0]
    weights = 2.0 / (degree * (degree + 1) * legendre_values**2)
    differences = gll_nodes[:, None] - gll_nodes[None, :] + np.eye(degree + 1)
    derivative = legendre_values[:, None] / legendre_values[None, :] / differences
    derivative = derivative * (1.0 - np.eye(degree + 1))
    derivative[0, 0] = -degree * (degree + 1) / 4.0
    derivative[degree, degree] = degree * (degree + 1) / 4.0
    return (weights, derivative)


def fold_rims(extended, dimension, points):
    length = extended.shape[dimension] - 2
    center = lax.slice_in_dim(extended, 1, length + 1, axis=dimension)
    upper_side = lax.slice_in_dim(extended, 2, length + 2, axis=dimension)
    lower_side = lax.slice_in_dim(extended, 0, length, axis=dimension)
    shape_ones = [1] * extended.ndim
    shape_ones[dimension] = length
    position = (jnp.arange(length, dtype=jnp.int32) % points).reshape(tuple(shape_ones))
    upper_flag = (position == points - 1).astype(extended.dtype)
    lower_flag = (position == 0).astype(extended.dtype)
    return center + upper_flag * upper_side + lower_flag * lower_side


def assemble_lattice(lattice, points):
    extended = extended_2(lattice, (("gx", 1),), 1)
    folded = fold_rims(extended, 1, points)
    extended = extended_2(folded, (("gy", 2),), 1)
    folded = fold_rims(extended, 2, points)
    extended = extended_2(folded, (("gz", 3),), 1)
    return fold_rims(extended, 3, points)


def along_first(lattice, matrix, points):
    blocked = lattice.reshape(
        lattice.shape[0], lattice.shape[1] // points, points, lattice.shape[2], lattice.shape[3]
    )
    result = jnp.einsum("ai,cpiyz->cpayz", matrix, blocked, precision=lax.Precision.HIGHEST)
    return result.reshape(lattice.shape)


def along_second(lattice, matrix, points):
    blocked = lattice.reshape(
        lattice.shape[0], lattice.shape[1], lattice.shape[2] // points, points, lattice.shape[3]
    )
    result = jnp.einsum("ai,cxpiz->cxpaz", matrix, blocked, precision=lax.Precision.HIGHEST)
    return result.reshape(lattice.shape)


def along_third(lattice, block_table):
    return jnp.dot(
        lattice, block_table, precision=lax.Precision.HIGHEST, preferred_element_type=jnp.float32
    )


def helmholtz(lattice, geometry, weighted, mass, tables, points):
    forward, backward, forward_third, backward_third = tables
    slope_first = along_first(lattice, forward, points)
    slope_second = along_second(lattice, forward, points)
    slope_third = along_third(lattice, forward_third)
    flux_first = weighted * (
        geometry[0] * slope_first + geometry[3] * slope_second + geometry[4] * slope_third
    )
    flux_second = weighted * (
        geometry[3] * slope_first + geometry[1] * slope_second + geometry[5] * slope_third
    )
    flux_third = weighted * (
        geometry[4] * slope_first + geometry[5] * slope_second + geometry[2] * slope_third
    )
    return (
        along_first(flux_first, backward, points)
        + along_second(flux_second, backward, points)
        + along_third(flux_third, backward_third)
        + mass * lattice
    )


def shards(right_side, geometry, viscosity, eig_low, eig_high, element_slot, dirichlet):
    points = DEGREE + 1
    weights, derivative = gll_tables(DEGREE)
    components = right_side.shape[0]
    size_first, size_second, size_third = viscosity.shape
    blocks_first = size_first // points
    blocks_second = size_second // points
    blocks_third = size_third // points
    forward = jnp.asarray(derivative, jnp.float32)
    backward = forward.T
    squared = forward * forward
    identity_third = jnp.eye(blocks_third, dtype=jnp.float32)
    tables = (
        forward,
        backward,
        jnp.kron(identity_third, backward),
        jnp.kron(identity_third, forward),
    )
    weight_table = jnp.asarray(weights, jnp.float32)
    diagonal_table = jnp.diagonal(forward)
    quadrature = (
        jnp.tile(weight_table, blocks_first)[:, None, None]
        * jnp.tile(weight_table, blocks_second)[None, :, None]
        * jnp.tile(weight_table, blocks_third)[None, None, :]
    )
    weighted = quadrature * viscosity
    determinant = (
        geometry[0] * (geometry[1] * geometry[2] - geometry[5] * geometry[5])
        - geometry[3] * (geometry[3] * geometry[2] - geometry[5] * geometry[4])
        + geometry[4] * (geometry[3] * geometry[5] - geometry[1] * geometry[4])
    )
    mass = helm_coefficient * quadrature * determinant
    end_first = jnp.tile(diagonal_table, blocks_first)[:, None, None]
    end_second = jnp.tile(diagonal_table, blocks_second)[None, :, None]
    end_third = jnp.tile(diagonal_table, blocks_third)[None, None, :]
    cross = (
        2.0
        * weighted
        * (
            end_first * end_second * geometry[3]
            + end_first * end_third * geometry[4]
            + end_second * end_third * geometry[5]
        )
    )
    diagonal_local = (
        (
            along_first((weighted * geometry[0])[None], squared.T, points)
            + along_second((weighted * geometry[1])[None], squared.T, points)
            + along_third((weighted * geometry[2])[None], jnp.kron(identity_third, squared))
        )[0]
        + cross
        + mass
    )
    slot_bricks = element_slot[0]
    elements = slot_bricks.shape[0]
    slot_index = jnp.arange(elements, dtype=jnp.int32)
    inverse = jnp.sum(
        jnp.where(slot_bricks[:, None] == slot_index[None, :], slot_index[:, None], 0), axis=0
    )
    bricks = jnp.take(right_side, inverse, axis=2)
    rhs_lattice = (
        bricks.reshape(
            components, points, points, points, blocks_first, blocks_second, blocks_third
        )
        .transpose(0, 4, 1, 5, 2, 6, 3)
        .reshape(components, size_first, size_second, size_third)
    )
    row_index = lax.axis_index("gx")
    low_plane = jnp.where(row_index == 0, dirichlet[0], 0).astype(jnp.float32)
    high_plane = jnp.where(row_index == lax.axis_size("gx") - 1, dirichlet[1], 0).astype(
        jnp.float32
    )
    middle = jnp.zeros((components, size_first - 2, size_second, size_third), jnp.float32)
    indicator = jnp.concatenate([low_plane[:, None], middle, high_plane[:, None]], axis=1)
    stacked = jnp.concatenate([rhs_lattice, diagonal_local[None], indicator], axis=0)
    assembled = assemble_lattice(stacked, points)
    keep = jnp.where(assembled[components + 1 :] > 0.5, 0.0, 1.0).astype(jnp.float32)
    residual = keep * assembled[:components]
    scaling = keep / assembled[components][None]
    midpoint = (eig_high[0] + eig_low[0]) * 0.5
    halfwidth = (eig_high[0] - eig_low[0]) * 0.5
    ratio_start = midpoint / halfwidth
    damping = 1.0 / ratio_start
    direction = scaling * residual / midpoint
    solution = jnp.zeros_like(residual)
    for iteration in range(ITERS):
        solution = solution + direction
        if iteration < ITERS - 1:
            image = assemble_lattice(
                helmholtz(direction, geometry, weighted, mass, tables, points), points
            )
            residual = residual - keep * image
            damping_next = 1.0 / (2.0 * ratio_start - damping)
            direction = damping_next * damping * direction + 2.0 * damping_next / halfwidth * (
                scaling * residual
            )
            damping = damping_next
    back_bricks = (
        solution.reshape(
            components, blocks_first, points, blocks_second, points, blocks_third, points
        )
        .transpose(0, 2, 4, 6, 1, 3, 5)
        .reshape(components, points * points * points, elements)
    )
    return jnp.take(back_bricks, slot_bricks, axis=2)


def solution(mesh):
    return jax.shard_map(
        shards,
        mesh=mesh,
        in_specs=(
            P(None, None, ("gx", "gy", "gz")),
            P(None, "gx", "gy", "gz"),
            P("gx", "gy", "gz"),
            P(),
            P(),
            P(("gx", "gy", "gz"), None),
            P(None, None, "gy", "gz"),
        ),
        out_specs=P(None, None, ("gx", "gy", "gz")),
        check_vma=False,
    )
```

profile of v0, /device:TPU:55, one launch (start us, length us, event | category | flops | bytes accessed | tf_op | source)
XLA Modules:
  0.0 154.8 jit_solution(15822499413609710861)
XLA Ops:
  14.0 2.9 %copy.139 = f32[3,1,8,2,8,16,8]{6,5,2,4,3,0,1:T(8,128)S(1)} copy(f32[3,1,8,2,8,16,8]{5,3,6,4,2,0,1:T(2,128)} %bitcast.171) | data formatting | bytes 393216 | tf_op jit(solution)/shard_map/reshape | solution.py:188
  19.1 2.3 %broadcast_multiply_fusion = (f32[16,8,16,8]{3,2,1,0:T(8,128)S(1)}, f32[16,8,16,8]{3,2,1,0:T(8,128)S(1)}, f32[16,8,16,8]{3,2,1,0:T(8,128)}) fusion(f32[8,8]{1,0:T(8,128)S(1)} %copy-done.1, f32[16,16]{1,0:T(8,128)} %fusion.106, f32[8,8]{1,0:T(8,128)} %constant.109, f32[8,8]{1,0:T(8,128)} %constant.125), kind=kLoop, calls=%fused_computation.24 | loop fusion | flops 49152 | bytes 198400 | tf_op jit(solution)/shard_map/jit(kron)/mul | solution.py:139
  23.8 18.2 %collective-permute-start = (f32[7,1,16,128]{3,1,2,0:T(1,128)S(1)}, f32[7,1,16,128]{3,1,2,0:T(1,128)S(1)}, u32[]{:S(2)}, u32[]{:S(2)}) collective-permute-start(f32[7,1,16,128]{3,1,2,0:T(1,128)S(1)} %get-tuple-element.16), channel_id=1, source_target_pairs={{64,0},{128,64},{192,128},{256,192},{320,256},{384,320},{448,384},... | collective-permute-start | bytes 172040 | tf_op jit(solution)/shard_map/ppermute | solution.py:22
  45.7 6.3 %collective-permute-done.1 = f32[7,1,16,128]{3,1,2,0:T(1,128)S(1)} collective-permute-done((f32[7,1,16,128]{3,1,2,0:T(1,128)S(1)}, f32[7,1,16,128]{3,1,2,0:T(1,128)S(1)}, u32[]{:S(2)}, u32[]{:S(2)}) %collective-permute-start.1) | collective-permute-done | bytes 57376 | tf_op jit(solution)/shard_map/ppermute | solution.py:21
  52.4 3.0 %collective-permute-start.2 = (f32[7,8,1,128]{3,1,2,0:T(8,128)S(1)}, f32[7,8,1,128]{3,1,2,0:T(8,128)S(1)}, u32[]{:S(2)}, u32[]{:S(2)}) collective-permute-start(f32[7,8,1,128]{3,1,2,0:T(8,128)S(1)} %get-tuple-element.14), channel_id=1, source_target_pairs={{8,0},{16,8},{24,16},{32,24},{40,32},{48,40},{56,48},{9,1},{17,9},... | collective-permute-start | bytes 86024 | tf_op jit(solution)/shard_map/ppermute | solution.py:22
  55.4 2.3 %collective-permute-start.3 = (f32[7,8,1,128]{3,1,2,0:T(8,128)S(1)}, f32[7,8,1,128]{3,1,2,0:T(8,128)S(1)}, u32[]{:S(2)}, u32[]{:S(2)}) collective-permute-start(f32[7,8,1,128]{3,1,2,0:T(8,128)S(1)} %get-tuple-element.15), channel_id=1, source_target_pairs={{0,8},{8,16},{16,24},{24,32},{32,40},{40,48},{48,56},{1,9},{9,17},... | collective-permute-start | bytes 86024 | tf_op jit(solution)/shard_map/ppermute | solution.py:21
  57.7 2.3 %collective-permute-done.3 = f32[7,8,1,128]{3,1,2,0:T(8,128)S(1)} collective-permute-done((f32[7,8,1,128]{3,1,2,0:T(8,128)S(1)}, f32[7,8,1,128]{3,1,2,0:T(8,128)S(1)}, u32[]{:S(2)}, u32[]{:S(2)}) %collective-permute-start.3) | collective-permute-done | bytes 28704 | tf_op jit(solution)/shard_map/ppermute | solution.py:21
  61.2 5.4 %collective-permute-start.4 = (f32[7,8,16,1]{3,1,2,0:T(8,128)}, f32[7,8,16,1]{3,1,2,0:T(8,128)}, u32[]{:S(2)}, u32[]{:S(2)}) collective-permute-start(f32[7,8,16,1]{3,1,2,0:T(8,128)} %get-tuple-element.12), channel_id=1, source_target_pairs={{1,0},{2,1},{3,2},{4,3},{5,4},{6,5},{7,6},{9,8},{10,9},{11,10},{12... | collective-permute-start | bytes 10760 | tf_op jit(solution)/shard_map/ppermute | solution.py:22
  66.6 3.5 %collective-permute-start.5 = (f32[7,8,16,1]{3,1,2,0:T(8,128)}, f32[7,8,16,1]{3,1,2,0:T(8,128)}, u32[]{:S(2)}, u32[]{:S(2)}) collective-permute-start(f32[7,8,16,1]{3,1,2,0:T(8,128)} %get-tuple-element.13), channel_id=1, source_target_pairs={{0,1},{1,2},{2,3},{3,4},{4,5},{5,6},{6,7},{8,9},{9,10},{10,11},{11... | collective-permute-start | bytes 10760 | tf_op jit(solution)/shard_map/ppermute | solution.py:21
  72.5 2.2 %collective-permute-done.4 = f32[7,8,16,1]{3,1,2,0:T(8,128)} collective-permute-done((f32[7,8,16,1]{3,1,2,0:T(8,128)}, f32[7,8,16,1]{3,1,2,0:T(8,128)}, u32[]{:S(2)}, u32[]{:S(2)}) %collective-permute-start.4) | collective-permute-done | bytes 3616 | tf_op jit(solution)/shard_map/ppermute | solution.py:22
  79.9 3.6 %collective-permute-start.6 = (f32[3,1,16,128]{3,1,2,0:T(1,128)S(1)}, f32[3,1,16,128]{3,1,2,0:T(1,128)S(1)}, u32[]{:S(2)}, u32[]{:S(2)}) collective-permute-start(f32[3,1,16,128]{3,1,2,0:T(1,128)S(1)} %get-tuple-element.34), channel_id=1, source_target_pairs={{64,0},{128,64},{192,128},{256,192},{320,256},{384,320},{448,384},... | collective-permute-start | bytes 73736 | tf_op jit(solution)/shard_map/ppermute | solution.py:22
  83.5 5.5 %collective-permute-start.7 = (f32[3,1,16,128]{3,1,2,0:T(1,128)S(1)}, f32[3,1,16,128]{3,1,2,0:T(1,128)S(1)}, u32[]{:S(2)}, u32[]{:S(2)}) collective-permute-start(f32[3,1,16,128]{3,1,2,0:T(1,128)S(1)} %get-tuple-element.35), channel_id=1, source_target_pairs={{0,64},{64,128},{128,192},{192,256},{256,320},{320,384},{384,448},... | collective-permute-start | bytes 73736 | tf_op jit(solution)/shard_map/ppermute | solution.py:21
  89.1 4.1 %collective-permute-done.7 = f32[3,1,16,128]{3,1,2,0:T(1,128)S(1)} collective-permute-done((f32[3,1,16,128]{3,1,2,0:T(1,128)S(1)}, f32[3,1,16,128]{3,1,2,0:T(1,128)S(1)}, u32[]{:S(2)}, u32[]{:S(2)}) %collective-permute-start.7) | collective-permute-done | bytes 24608 | tf_op jit(solution)/shard_map/ppermute | solution.py:21
  93.3 3.0 %collective-permute-start.8 = (f32[3,8,1,128]{3,1,2,0:T(8,128)S(1)}, f32[3,8,1,128]{3,1,2,0:T(8,128)S(1)}, u32[]{:S(2)}, u32[]{:S(2)}) collective-permute-start(f32[3,8,1,128]{3,1,2,0:T(8,128)S(1)} %get-tuple-element.32), channel_id=1, source_target_pairs={{8,0},{16,8},{24,16},{32,24},{40,32},{48,40},{56,48},{9,1},{17,9},... | collective-permute-start | bytes 36872 | tf_op jit(solution)/shard_map/ppermute | solution.py:22
  96.3 2.3 %collective-permute-start.9 = (f32[3,8,1,128]{3,1,2,0:T(8,128)S(1)}, f32[3,8,1,128]{3,1,2,0:T(8,128)S(1)}, u32[]{:S(2)}, u32[]{:S(2)}) collective-permute-start(f32[3,8,1,128]{3,1,2,0:T(8,128)S(1)} %get-tuple-element.33), channel_id=1, source_target_pairs={{0,8},{8,16},{16,24},{24,32},{32,40},{40,48},{48,56},{1,9},{9,17},... | collective-permute-start | bytes 36872 | tf_op jit(solution)/shard_map/ppermute | solution.py:21
  98.6 2.2 %collective-permute-done.9 = f32[3,8,1,128]{3,1,2,0:T(8,128)S(1)} collective-permute-done((f32[3,8,1,128]{3,1,2,0:T(8,128)S(1)}, f32[3,8,1,128]{3,1,2,0:T(8,128)S(1)}, u32[]{:S(2)}, u32[]{:S(2)}) %collective-permute-start.9) | collective-permute-done | bytes 12320 | tf_op jit(solution)/shard_map/ppermute | solution.py:21
  101.0 2.3 %collective-permute-start.10 = (f32[3,8,16,1]{3,1,2,0:T(8,128)S(1)}, f32[3,8,16,1]{3,1,2,0:T(8,128)S(1)}, u32[]{:S(2)}, u32[]{:S(2)}) collective-permute-start(f32[3,8,16,1]{3,1,2,0:T(8,128)S(1)} %get-tuple-element.30), channel_id=1, source_target_pairs={{1,0},{2,1},{3,2},{4,3},{5,4},{6,5},{7,6},{9,8},{10,9},{11,10},{12... | collective-permute-start | bytes 4616 | tf_op jit(solution)/shard_map/ppermute | solution.py:22
  103.3 7.0 %collective-permute-start.11 = (f32[3,8,16,1]{3,1,2,0:T(8,128)S(1)}, f32[3,8,16,1]{3,1,2,0:T(8,128)S(1)}, u32[]{:S(2)}, u32[]{:S(2)}) collective-permute-start(f32[3,8,16,1]{3,1,2,0:T(8,128)S(1)} %get-tuple-element.31), channel_id=1, source_target_pairs={{0,1},{1,2},{2,3},{3,4},{4,5},{5,6},{6,7},{8,9},{9,10},{10,11},{11... | collective-permute-start | bytes 4616 | tf_op jit(solution)/shard_map/ppermute | solution.py:21
  117.2 7.3 %collective-permute-start.13 = (f32[3,1,16,128]{3,1,2,0:T(1,128)S(1)}, f32[3,1,16,128]{3,1,2,0:T(1,128)S(1)}, u32[]{:S(2)}, u32[]{:S(2)}) collective-permute-start(f32[3,1,16,128]{3,1,2,0:T(1,128)S(1)} %get-tuple-element.29), channel_id=1, source_target_pairs={{0,64},{64,128},{128,192},{192,256},{256,320},{320,384},{384,448},... | collective-permute-start | bytes 73736 | tf_op jit(solution)/shard_map/ppermute | solution.py:21
  126.7 3.3 %collective-permute-start.14 = (f32[3,8,1,128]{3,1,2,0:T(8,128)S(1)}, f32[3,8,1,128]{3,1,2,0:T(8,128)S(1)}, u32[]{:S(2)}, u32[]{:S(2)}) collective-permute-start(f32[3,8,1,128]{3,1,2,0:T(8,128)S(1)} %get-tuple-element.26), channel_id=1, source_target_pairs={{8,0},{16,8},{24,16},{32,24},{40,32},{48,40},{56,48},{9,1},{17,9},... | collective-permute-start | bytes 36872 | tf_op jit(solution)/shard_map/ppermute | solution.py:22
  132.0 2.4 %collective-permute-done.15 = f32[3,8,1,128]{3,1,2,0:T(8,128)S(1)} collective-permute-done((f32[3,8,1,128]{3,1,2,0:T(8,128)S(1)}, f32[3,8,1,128]{3,1,2,0:T(8,128)S(1)}, u32[]{:S(2)}, u32[]{:S(2)}) %collective-permute-start.15) | collective-permute-done | bytes 12320 | tf_op jit(solution)/shard_map/ppermute | solution.py:21
  136.5 7.0 %collective-permute-start.17 = (f32[3,8,16,1]{3,1,2,0:T(8,128)S(1)}, f32[3,8,16,1]{3,1,2,0:T(8,128)S(1)}, u32[]{:S(2)}, u32[]{:S(2)}) collective-permute-start(f32[3,8,16,1]{3,1,2,0:T(8,128)S(1)} %get-tuple-element.25), channel_id=1, source_target_pairs={{0,1},{1,2},{2,3},{3,4},{4,5},{5,6},{6,7},{8,9},{9,10},{10,11},{11... | collective-permute-start | bytes 4616 | tf_op jit(solution)/shard_map/ppermute | solution.py:21
  148.1 2.4 %copy.121 = f32[3,8,8,8,1,2,16]{6,5,3,2,1,0,4:T(2,128)} copy(f32[3,8,8,8,1,2,16]{3,6,2,5,1,0,4:T(8,128)S(1)} %bitcast.168) | data formatting | bytes 393216 | tf_op jit(solution)/shard_map/transpose | solution.py:224
  150.5 2.3 %reshape.391 = f32[3,512,32]{2,1,0:T(8,128)S(1)} reshape(f32[3,8,8,8,1,2,16]{6,5,3,2,1,0,4:T(2,128)} %copy.121) | data formatting | bytes 393216 | tf_op jit(solution)/shard_map/reshape | solution.py:225
  (144 shorter events, 49.2 us)
Async XLA Ops:
  0.0 10.7 %copy-start = (f32[3,512,32]{1,2,0:T(8,128)S(1)}, f32[3,512,32]{1,2,0:T(8,128)}, u32[]{:S(2)}) copy-start(f32[3,512,32]{1,2,0:T(8,128)} %param.11) | copy-start | bytes 589828
  8.2 15.1 %copy-start.3 = (f32[1,8,16,128]{3,2,1,0:T(8,128)}, f32[1,8,16,128]{3,2,1,0:T(8,128)S(1)}, u32[]{:S(2)}) copy-start(f32[1,8,16,128]{3,2,1,0:T(8,128)S(1)} %get-tuple-element.23) | copy-start | bytes 196612
  23.8 21.9 %collective-permute-start = (f32[7,1,16,128]{3,1,2,0:T(1,128)S(1)}, f32[7,1,16,128]{3,1,2,0:T(1,128)S(1)}, u32[]{:S(2)}, u32[]{:S(2)}) collective-permute-start(f32[7,1,16,128]{3,1,2,0:T(1,128)S(1)} %get-tuple-element.16), channel_id=1, source_target_pairs={{64,0},{128,64},{192,128},{256,192},{320,256},{384,320},{448,384},... | collective-permute-start | bytes 172040 | tf_op jit(solution)/shard_map/ppermute | solution.py:22
  42.0 10.0 %collective-permute-start.1 = (f32[7,1,16,128]{3,1,2,0:T(1,128)S(1)}, f32[7,1,16,128]{3,1,2,0:T(1,128)S(1)}, u32[]{:S(2)}, u32[]{:S(2)}) collective-permute-start(f32[7,1,16,128]{3,1,2,0:T(1,128)S(1)} %get-tuple-element.17), channel_id=1, source_target_pairs={{0,64},{64,128},{128,192},{192,256},{256,320},{320,384},{384,448},... | collective-permute-start | bytes 172040 | tf_op jit(solution)/shard_map/ppermute | solution.py:21
  52.4 5.3 %collective-permute-start.2 = (f32[7,8,1,128]{3,1,2,0:T(8,128)S(1)}, f32[7,8,1,128]{3,1,2,0:T(8,128)S(1)}, u32[]{:S(2)}, u32[]{:S(2)}) collective-permute-start(f32[7,8,1,128]{3,1,2,0:T(8,128)S(1)} %get-tuple-element.14), channel_id=1, source_target_pairs={{8,0},{16,8},{24,16},{32,24},{40,32},{48,40},{56,48},{9,1},{17,9},... | collective-permute-start | bytes 86024 | tf_op jit(solution)/shard_map/ppermute | solution.py:22
  55.4 4.6 %collective-permute-start.3 = (f32[7,8,1,128]{3,1,2,0:T(8,128)S(1)}, f32[7,8,1,128]{3,1,2,0:T(8,128)S(1)}, u32[]{:S(2)}, u32[]{:S(2)}) collective-permute-start(f32[7,8,1,128]{3,1,2,0:T(8,128)S(1)} %get-tuple-element.15), channel_id=1, source_target_pairs={{0,8},{8,16},{16,24},{24,32},{32,40},{40,48},{48,56},{1,9},{9,17},... | collective-permute-start | bytes 86024 | tf_op jit(solution)/shard_map/ppermute | solution.py:21
  60.1 17.4 %copy-start.13 = (f32[8,8,1,1]{1,0,3,2:T(8,128)S(1)}, f32[8,8,1,1]{1,0,3,2:T(8,128)}, u32[]{:S(2)}) copy-start(f32[8,8,1,1]{1,0,3,2:T(8,128)} %constant.126) | copy-start | bytes 772
  60.1 17.8 %copy-start.14 = (f32[8,8,1,1,1]{1,0,4,3,2:T(8,128)S(1)}, f32[8,8,1,1,1]{1,0,4,3,2:T(8,128)}, u32[]{:S(2)}) copy-start(f32[8,8,1,1,1]{1,0,4,3,2:T(8,128)} %constant.127) | copy-start | bytes 772
  61.2 17.1 %copy-start.7 = (f32[8,16,128]{2,0,1:T(8,128)S(1)}, f32[8,16,128]{2,0,1:T(8,128)}, u32[]{:S(2)}) copy-start(f32[8,16,128]{2,0,1:T(8,128)} %get-tuple-element.39) | copy-start | bytes 196612
  61.2 13.5 %collective-permute-start.4 = (f32[7,8,16,1]{3,1,2,0:T(8,128)}, f32[7,8,16,1]{3,1,2,0:T(8,128)}, u32[]{:S(2)}, u32[]{:S(2)}) collective-permute-start(f32[7,8,16,1]{3,1,2,0:T(8,128)} %get-tuple-element.12), channel_id=1, source_target_pairs={{1,0},{2,1},{3,2},{4,3},{5,4},{6,5},{7,6},{9,8},{10,9},{11,10},{12... | collective-permute-start | bytes 10760 | tf_op jit(solution)/shard_map/ppermute | solution.py:22
  66.6 9.2 %collective-permute-start.5 = (f32[7,8,16,1]{3,1,2,0:T(8,128)}, f32[7,8,16,1]{3,1,2,0:T(8,128)}, u32[]{:S(2)}, u32[]{:S(2)}) collective-permute-start(f32[7,8,16,1]{3,1,2,0:T(8,128)} %get-tuple-element.13), channel_id=1, source_target_pairs={{0,1},{1,2},{2,3},{3,4},{4,5},{5,6},{6,7},{8,9},{9,10},{10,11},{11... | collective-permute-start | bytes 10760 | tf_op jit(solution)/shard_map/ppermute | solution.py:21
  79.9 9.2 %collective-permute-start.6 = (f32[3,1,16,128]{3,1,2,0:T(1,128)S(1)}, f32[3,1,16,128]{3,1,2,0:T(1,128)S(1)}, u32[]{:S(2)}, u32[]{:S(2)}) collective-permute-start(f32[3,1,16,128]{3,1,2,0:T(1,128)S(1)} %get-tuple-element.34), channel_id=1, source_target_pairs={{64,0},{128,64},{192,128},{256,192},{320,256},{384,320},{448,384},... | collective-permute-start | bytes 73736 | tf_op jit(solution)/shard_map/ppermute | solution.py:22
  83.5 9.7 %collective-permute-start.7 = (f32[3,1,16,128]{3,1,2,0:T(1,128)S(1)}, f32[3,1,16,128]{3,1,2,0:T(1,128)S(1)}, u32[]{:S(2)}, u32[]{:S(2)}) collective-permute-start(f32[3,1,16,128]{3,1,2,0:T(1,128)S(1)} %get-tuple-element.35), channel_id=1, source_target_pairs={{0,64},{64,128},{128,192},{192,256},{256,320},{320,384},{384,448},... | collective-permute-start | bytes 73736 | tf_op jit(solution)/shard_map/ppermute | solution.py:21
  93.3 5.3 %collective-permute-start.8 = (f32[3,8,1,128]{3,1,2,0:T(8,128)S(1)}, f32[3,8,1,128]{3,1,2,0:T(8,128)S(1)}, u32[]{:S(2)}, u32[]{:S(2)}) collective-permute-start(f32[3,8,1,128]{3,1,2,0:T(8,128)S(1)} %get-tuple-element.32), channel_id=1, source_target_pairs={{8,0},{16,8},{24,16},{32,24},{40,32},{48,40},{56,48},{9,1},{17,9},... | collective-permute-start | bytes 36872 | tf_op jit(solution)/shard_map/ppermute | solution.py:22
  96.3 4.5 %collective-permute-start.9 = (f32[3,8,1,128]{3,1,2,0:T(8,128)S(1)}, f32[3,8,1,128]{3,1,2,0:T(8,128)S(1)}, u32[]{:S(2)}, u32[]{:S(2)}) collective-permute-start(f32[3,8,1,128]{3,1,2,0:T(8,128)S(1)} %get-tuple-element.33), channel_id=1, source_target_pairs={{0,8},{8,16},{16,24},{24,32},{32,40},{40,48},{48,56},{1,9},{9,17},... | collective-permute-start | bytes 36872 | tf_op jit(solution)/shard_map/ppermute | solution.py:21
  101.0 10.5 %collective-permute-start.10 = (f32[3,8,16,1]{3,1,2,0:T(8,128)S(1)}, f32[3,8,16,1]{3,1,2,0:T(8,128)S(1)}, u32[]{:S(2)}, u32[]{:S(2)}) collective-permute-start(f32[3,8,16,1]{3,1,2,0:T(8,128)S(1)} %get-tuple-element.30), channel_id=1, source_target_pairs={{1,0},{2,1},{3,2},{4,3},{5,4},{6,5},{7,6},{9,8},{10,9},{11,10},{12... | collective-permute-start | bytes 4616 | tf_op jit(solution)/shard_map/ppermute | solution.py:22
  103.3 9.4 %collective-permute-start.11 = (f32[3,8,16,1]{3,1,2,0:T(8,128)S(1)}, f32[3,8,16,1]{3,1,2,0:T(8,128)S(1)}, u32[]{:S(2)}, u32[]{:S(2)}) collective-permute-start(f32[3,8,16,1]{3,1,2,0:T(8,128)S(1)} %get-tuple-element.31), channel_id=1, source_target_pairs={{0,1},{1,2},{2,3},{3,4},{4,5},{5,6},{6,7},{8,9},{9,10},{10,11},{11... | collective-permute-start | bytes 4616 | tf_op jit(solution)/shard_map/ppermute | solution.py:21
  113.0 11.4 %copy-start.21 = (s32[1,32]{1,0:T(1,128)S(1)}, s32[1,32]{1,0:T(1,128)}, u32[]{:S(2)}) copy-start(s32[1,32]{1,0:T(1,128)} %param.16) | copy-start | bytes 388
  115.2 9.2 %collective-permute-start.12 = (f32[3,1,16,128]{3,1,2,0:T(1,128)S(1)}, f32[3,1,16,128]{3,1,2,0:T(1,128)S(1)}, u32[]{:S(2)}, u32[]{:S(2)}) collective-permute-start(f32[3,1,16,128]{3,1,2,0:T(1,128)S(1)} %get-tuple-element.28), channel_id=1, source_target_pairs={{64,0},{128,64},{192,128},{256,192},{320,256},{384,320},{448,384},... | collective-permute-start | bytes 73736 | tf_op jit(solution)/shard_map/ppermute | solution.py:22
  117.2 9.4 %collective-permute-start.13 = (f32[3,1,16,128]{3,1,2,0:T(1,128)S(1)}, f32[3,1,16,128]{3,1,2,0:T(1,128)S(1)}, u32[]{:S(2)}, u32[]{:S(2)}) collective-permute-start(f32[3,1,16,128]{3,1,2,0:T(1,128)S(1)} %get-tuple-element.29), channel_id=1, source_target_pairs={{0,64},{64,128},{128,192},{192,256},{256,320},{320,384},{384,448},... | collective-permute-start | bytes 73736 | tf_op jit(solution)/shard_map/ppermute | solution.py:21
  126.7 5.3 %collective-permute-start.14 = (f32[3,8,1,128]{3,1,2,0:T(8,128)S(1)}, f32[3,8,1,128]{3,1,2,0:T(8,128)S(1)}, u32[]{:S(2)}, u32[]{:S(2)}) collective-permute-start(f32[3,8,1,128]{3,1,2,0:T(8,128)S(1)} %get-tuple-element.26), channel_id=1, source_target_pairs={{8,0},{16,8},{24,16},{32,24},{40,32},{48,40},{56,48},{9,1},{17,9},... | collective-permute-start | bytes 36872 | tf_op jit(solution)/shard_map/ppermute | solution.py:22
  129.9 4.4 %collective-permute-start.15 = (f32[3,8,1,128]{3,1,2,0:T(8,128)S(1)}, f32[3,8,1,128]{3,1,2,0:T(8,128)S(1)}, u32[]{:S(2)}, u32[]{:S(2)}) collective-permute-start(f32[3,8,1,128]{3,1,2,0:T(8,128)S(1)} %get-tuple-element.27), channel_id=1, source_target_pairs={{0,8},{8,16},{16,24},{24,32},{32,40},{40,48},{48,56},{1,9},{9,17},... | collective-permute-start | bytes 36872 | tf_op jit(solution)/shard_map/ppermute | solution.py:21
  134.6 10.3 %collective-permute-start.16 = (f32[3,8,16,1]{3,1,2,0:T(8,128)S(1)}, f32[3,8,16,1]{3,1,2,0:T(8,128)S(1)}, u32[]{:S(2)}, u32[]{:S(2)}) collective-permute-start(f32[3,8,16,1]{3,1,2,0:T(8,128)S(1)} %get-tuple-element.24), channel_id=1, source_target_pairs={{1,0},{2,1},{3,2},{4,3},{5,4},{6,5},{7,6},{9,8},{10,9},{11,10},{12... | collective-permute-start | bytes 4616 | tf_op jit(solution)/shard_map/ppermute | solution.py:22
  136.5 9.6 %collective-permute-start.17 = (f32[3,8,16,1]{3,1,2,0:T(8,128)S(1)}, f32[3,8,16,1]{3,1,2,0:T(8,128)S(1)}, u32[]{:S(2)}, u32[]{:S(2)}) collective-permute-start(f32[3,8,16,1]{3,1,2,0:T(8,128)S(1)} %get-tuple-element.25), channel_id=1, source_target_pairs={{0,1},{1,2},{2,3},{3,4},{4,5},{5,6},{6,7},{8,9},{9,10},{10,11},{11... | collective-permute-start | bytes 4616 | tf_op jit(solution)/shard_map/ppermute | solution.py:21
  (16 other events, 67.5 us)
where the time goes:
time: 156 us; the launch traced here: 155 us
  starting transfers between devices  81.4 us (52%)
  waiting for transfers between devices  27.5 us (18%)
  local copies, waits for them, and re-layouts  26.2 us (17%)
  other arithmetic  11.9 us (8%)
  matrix products  5.33 us (3%)
  between operations  2.45 us (2%)
    ppermute x9, starting transfers between devices, extended_2(): after = lax.ppermute(first, axis, down)  42.6 us
    ppermute x9, starting transfers between devices, extended_2(): before = lax.ppermute(last, axis, up)  38.8 us
    ppermute x9, waiting for transfers between devices, extended_2(): before = lax.ppermute(last, axis, up)  22.9 us
    reshape x2, local copies, waits for them, and re-layouts, shards(): rhs_lattice = bricks.reshape(components, points, points, points, blocks_f...  4.99 us
    ppermute x9, waiting for transfers between devices, extended_2(): after = lax.ppermute(first, axis, down)  4.61 us
  transfers between devices with their start and end apart: 18, of which 12 were waited for; matrix products, arithmetic and copies ran while one was open for 2% of the time, Pallas kernels for 0%

commit v1 on v0

v1 whole, which is shorter than its diff:
```python
import functools

import jax
import jax.numpy as jnp
import numpy as np
from jax import lax
from jax.experimental import pallas as pl
from jax.experimental.pallas import tpu as pltpu
from jax.sharding import PartitionSpec as P

DEGREE = 7
HELM = 10.0
N_FIRST = 5
MESH = pl.DeviceIdType.MESH

SIDES = ((-1, 0), (1, 0), (0, -1), (0, 1), (-1, -1), (-1, 1), (1, -1), (1, 1))


def legendre_pair(values, degree):
    previous = 0.0 * values + 1.0
    current = values.copy()
    for order in range(2, degree + 1):
        previous, current = (
            current,
            ((2 * order - 1) * values * current - (order - 1) * previous) / order,
        )
    return (current, previous)


def gll_tables(degree):
    start = np.cos(np.pi * np.arange(degree + 1) / degree)
    nodes_now = start.copy()
    for sweep in range(80):
        top_value, lower_value = legendre_pair(nodes_now, degree)
        nodes_now = nodes_now - (nodes_now * top_value - lower_value) / ((degree + 1) * top_value)
    gll_nodes = nodes_now[::-1].copy()
    gll_nodes[0] = -1.0
    gll_nodes[degree] = 1.0
    legendre_values = legendre_pair(gll_nodes, degree)[0]
    weights = 2.0 / (degree * (degree + 1) * legendre_values**2)
    differences = gll_nodes[:, None] - gll_nodes[None, :] + np.eye(degree + 1)
    derivative = legendre_values[:, None] / legendre_values[None, :] / differences
    derivative = derivative * (1.0 - np.eye(degree + 1))
    derivative[0, 0] = -degree * (degree + 1) / 4.0
    derivative[degree, degree] = degree * (degree + 1) / 4.0
    return (weights, derivative)


WEIGHTS, DERIVATIVE = gll_tables(DEGREE)
DF = DERIVATIVE.astype(np.float32)
WF = WEIGHTS.astype(np.float32)
DS = DF * DF
ENDS = np.diagonal(DF)


def lane_table():
    sub = np.arange(8)
    tiles = []
    for matrix in (DF, DF.T, DS.T):
        for turn in range(8):
            tiles.append(np.repeat(matrix[sub, (sub - turn) % 8][:, None], 128, axis=1))
    lane = np.arange(128) % 8
    tiles.append(WF[:, None] * WF[lane][None, :])
    tiles.append(2.0 * ENDS[:, None] * ENDS[lane][None, :])
    tiles.append(np.repeat(2.0 * ENDS[:, None], 128, axis=1))
    tiles.append(np.repeat(2.0 * ENDS[lane][None, :], 8, axis=0))
    return np.stack(tiles).astype(np.float32)


def lane_matrices():
    import ml_dtypes

    out = []
    for matrix in (DF.T, DF, DS):
        wide = np.kron(np.eye(16, dtype=np.float32), matrix).astype(np.float32)
        high = wide.astype(ml_dtypes.bfloat16)
        low = (wide - high.astype(np.float32)).astype(ml_dtypes.bfloat16)
        half = np.concatenate([high, low], axis=1)
        out.append(np.concatenate([half, half], axis=0))
    return np.stack(out)


def halves(x):
    high = x.astype(jnp.bfloat16)
    low = (x - high.astype(jnp.float32)).astype(jnp.bfloat16)
    return high, low


def slot_matrix(slot):
    row = lax.broadcasted_iota(jnp.int32, (32, 32), 0)
    element = (row & 16) + ((16 - (row & 15)) & 15)
    return jnp.where(jnp.broadcast_to(slot, (32, 32)) == element, 1.0, 0.0).astype(jnp.float32)


def turn_columns(a, b, down):
    sub = lax.broadcasted_iota(jnp.int32, a.shape, 1)
    group = lax.broadcasted_iota(jnp.int32, a.shape, 2) // 8
    for bit in (1, 2, 4):
        here = (group & bit) != 0
        if down:
            ra, rb = pltpu.roll(a, bit, 1), pltpu.roll(b, bit, 1)
            na, nb = jnp.where(sub < bit, rb, ra), jnp.where(sub < bit, ra, rb)
        else:
            ra, rb = pltpu.roll(a, 8 - bit, 1), pltpu.roll(b, 8 - bit, 1)
            na, nb = jnp.where(sub < 8 - bit, ra, rb), jnp.where(sub < 8 - bit, rb, ra)
        a, b = jnp.where(here, na, a), jnp.where(here, nb, b)
    here = (group & 8) != 0
    return jnp.where(here, b, a), jnp.where(here, a, b)


def lane_turn(x, left):
    if not left:
        return pltpu.roll(x, 0, 1, stride=8, stride_axis=0)
    row = lax.broadcasted_iota(jnp.int32, x.shape, 0)
    for bit in (1, 2, 4, 8):
        x = jnp.where((row & bit) != 0, pltpu.roll(x, 128 - 8 * bit, 1), x)
    return x


def along_first(matrix, field):
    planes = [field[2 * i : 2 * i + 2] for i in range(8)]
    out = []
    for a in range(8):
        total = None
        for i in range(8):
            if abs(matrix[a, i]) > 0:
                term = planes[i] * float(matrix[a, i])
                total = term if total is None else total + term
        out.append(total)
    return jnp.concatenate(out, axis=0)


def along_second(tab, base, field):
    total = field * tab[base]
    for turn in range(1, 8):
        total = total + pltpu.roll(field, turn, 1) * tab[base + turn]
    return total


def along_third(matrix, field):
    high, low = halves(field.reshape(128, 128))
    both = jnp.dot(
        jnp.concatenate([high, low], axis=1), matrix, preferred_element_type=jnp.float32
    )
    return (both[:, :128] + both[:, 128:]).reshape(16, 8, 128)


def fold_lanes(field):
    lane = lax.broadcasted_iota(jnp.int32, field.shape, 2)
    upper = (lane % 8 == 7) & (lane < 127)
    lower = (lane % 8 == 0) & (lane > 0)
    return (
        field
        + jnp.where(upper, pltpu.roll(field, 127, 2), 0.0)
        + jnp.where(lower, pltpu.roll(field, 1, 2), 0.0)
    )


def kernel(
    sizes,
    rs_h, geo_h, vis_h, low_s, high_s, slot_h, dir_h, tab_h, mat_h,
    out,
    rs, geo, vis, slot, dirs, tab, mats, gw, mass, inv, scale, zed, way, flux,
    v0, v1, v2, ysend, zsend, yrecv, zrecv, xrecv,
    in_sem, ysem, yrsem, zsem, zrsem, xsem, xrsem,
):
    n_gx, n_gy, n_gz = sizes
    gx, gy, gz = lax.axis_index("gx"), lax.axis_index("gy"), lax.axis_index("gz")

    loads = [
        pltpu.make_async_copy(src, dst, in_sem.at[k])
        for k, (src, dst) in enumerate(
            (
                (rs_h, rs),
                (slot_h, slot),
                (geo_h, geo),
                (vis_h, vis),
                (tab_h, tab),
                (mat_h, mats),
                (dir_h, dirs),
            )
        )
    ]
    for load in loads:
        load.start()

    def inside(step_y, step_z):
        ok = None
        for step, at, size in ((step_y, gy, n_gy), (step_z, gz, n_gz)):
            if step:
                here = (at + step >= 0) & (at + step < size)
                ok = here if ok is None else ok & here
        return ok

    def device(step_y, step_z):
        return {"gx": gx, "gy": gy + step_y, "gz": gz + step_z}

    yrecv[...] = jnp.zeros_like(yrecv)
    zrecv[...] = jnp.zeros_like(zrecv)
    xrecv[...] = jnp.zeros_like(xrecv)

    barrier = pltpu.get_barrier_semaphore()
    count = 0
    for step_y, step_z in SIDES:
        here = inside(step_y, step_z)
        count = count + jnp.where(here, 1, 0)

        @pl.when(here)
        def _():
            pl.semaphore_signal(
                barrier, inc=1, device_id=device(step_y, step_z), device_id_type=MESH
            )

    for step in (-1, 1):
        here = (gx + step >= 0) & (gx + step < n_gx)
        count = count + jnp.where(here, 1, 0)

        @pl.when(here)
        def _():
            pl.semaphore_signal(
                barrier,
                inc=1,
                device_id={"gx": gx + step, "gy": gy, "gz": gz},
                device_id_type=MESH,
            )

    def side_copy(rnd, side, fields):
        step_y, step_z = SIDES[side]
        back = SIDES.index((-step_y, -step_z))
        if side < 2:
            part = (pl.ds(0, fields),)
            return lambda to: pltpu.make_async_remote_copy(
                src_ref=ysend.at[(rnd, side) + part],
                dst_ref=yrecv.at[(rnd, back if to else side) + part],
                send_sem=ysem.at[rnd, side],
                recv_sem=yrsem.at[rnd, back if to else side],
                device_id=device(step_y, step_z),
                device_id_type=MESH,
            )
        part = (pl.ds(0, 2 if fields > 3 else 1),)
        return lambda to: pltpu.make_async_remote_copy(
            src_ref=zsend.at[(rnd,) + part],
            dst_ref=zrecv.at[(rnd, (back if to else side) - 2) + part],
            send_sem=zsem.at[rnd, side - 2],
            recv_sem=zrsem.at[rnd, (back if to else side) - 2],
            device_id=device(step_y, step_z),
            device_id_type=MESH,
        )

    def first_copy(rnd, v, side, fields, to):
        step = (-1, 1)[side]
        plane = (0, 112)[side]
        return pltpu.make_async_remote_copy(
            src_ref=v.at[pl.ds(0, fields), pl.ds(plane, 16)],
            dst_ref=xrecv.at[rnd, (1 - side) if to else side, pl.ds(0, fields)],
            send_sem=xsem.at[rnd, side],
            recv_sem=xrsem.at[rnd, (1 - side) if to else side],
            device_id={"gx": gx + step, "gy": gy, "gz": gz},
            device_id_type=MESH,
        )

    def packed(v, fields):
        lane = lax.broadcasted_iota(jnp.int32, (8, 128), 1) // 2
        groups = [[(f, t) for f in range(3) for t in range(16)]]
        if fields > 3:
            groups.append([(3, t) for t in range(16)] + [(4, t) for t in range(6)])
        for n, group in enumerate(groups):
            parts = [None] * 4
            for q, (f, t) in enumerate(group):
                moved = pltpu.roll(v[f, pl.ds(8 * t, 8), :], 2 * q + 1, 1)
                old = parts[q % 4]
                parts[q % 4] = moved if old is None else jnp.where(lane == q, moved, old)
            for k in range(1, 4):
                parts[0] = jnp.where(lane % 4 == k, parts[k], parts[0])
            yield n, group, parts[0]

    def exchange(rnd, v, fields, x_fields):
        for f in range(fields):
            row7, row8 = v[f, pl.ds(7, 8, stride=16), :], v[f, pl.ds(8, 8, stride=16), :]
            v[f, pl.ds(7, 8, stride=16), :] = row7 + row8
            v[f, pl.ds(8, 8, stride=16), :] = row7 + row8
            ysend[rnd, 0, f] = v[f, pl.ds(0, 8, stride=16), :]
            ysend[rnd, 1, f] = v[f, pl.ds(15, 8, stride=16), :]
        groups = []
        for n, group, tile in packed(v, fields):
            zsend[rnd, n] = tile
            groups.append(group)
        if rnd == 0:
            pl.semaphore_wait(barrier, count)
        for side, (step_y, step_z) in enumerate(SIDES):

            @pl.when(inside(step_y, step_z))
            def _():
                side_copy(rnd, side, fields)(True).start()

        for side, (step_y, step_z) in enumerate(SIDES):

            @pl.when(inside(step_y, step_z))
            def _():
                side_copy(rnd, side, fields)(False).wait_recv()

        lane = lax.broadcasted_iota(jnp.int32, (8, 128), 1)
        sub = lax.broadcasted_iota(jnp.int32, (8, 128), 0)
        odd = lane % 2 == 1
        rim = (lane == 0) | (lane == 127)

        def swapped(minus, plus):
            return jnp.where(odd, pltpu.roll(minus, 1, 1), pltpu.roll(plus, 127, 1))

        for n, group in enumerate(groups):
            near = swapped(zrecv[rnd, 0, n], zrecv[rnd, 1, n])
            below = swapped(zrecv[rnd, 2, n], zrecv[rnd, 3, n])
            above = swapped(zrecv[rnd, 4, n], zrecv[rnd, 5, n])
            below = pltpu.roll(pltpu.roll(below, 1, 0), 126, 1)
            above = pltpu.roll(pltpu.roll(above, 7, 0), 2, 1)
            upper_tile = (lane // 2) % 2 == 1
            near = near + jnp.where((sub == 0) & ~upper_tile, below, 0.0)
            near = near + jnp.where((sub == 7) & upper_tile, above, 0.0)
            order = sorted(range(len(group)), key=lambda q: group[q][1] not in (0, 1, 14, 15))
            for q in order:
                f, t = group[q]
                moved = pltpu.roll(near, (128 - (2 * q + 1)) % 128, 1)
                v[f, pl.ds(8 * t, 8), :] = v[f, pl.ds(8 * t, 8), :] + jnp.where(rim, moved, 0.0)
        for f in range(fields):
            for side, row in ((0, 0), (1, 15)):
                rows = pl.ds(row, 8, stride=16)
                v[f, rows, :] = v[f, rows, :] + yrecv[rnd, side, f]
        for side, step in enumerate((-1, 1)):

            @pl.when((gx + step >= 0) & (gx + step < n_gx))
            def _():
                first_copy(rnd, v, side, x_fields, True).start()

    def arrive(rnd, v, x_fields):
        for side, step in enumerate((-1, 1)):

            @pl.when((gx + step >= 0) & (gx + step < n_gx))
            def _():
                first_copy(rnd, v, side, x_fields, False).wait_recv()

    def field_of(v, f):
        return v[f].reshape(16, 8, 128)

    def whole(rnd, v, f):
        own = field_of(v, f)
        return jnp.concatenate(
            [
                own[:2] + xrecv[rnd, 0, f].reshape(2, 8, 128),
                own[2:14],
                own[14:] + xrecv[rnd, 1, f].reshape(2, 8, 128),
            ],
            axis=0,
        )

    loads[0].wait()
    loads[1].wait()
    one_hot = slot_matrix(slot[...]).astype(jnp.bfloat16)
    pair = jnp.concatenate([one_hot, one_hot], axis=1)
    blocks = []
    for c in range(3):
        high, low = halves(rs[c])
        placed = jnp.dot(
            pair, jnp.concatenate([high, low], axis=0), preferred_element_type=jnp.float32
        )
        for ip in range(4):
            blocks.append(placed[:, 128 * ip : 128 * ip + 128])
    rows = lane_turn(jnp.concatenate(blocks, axis=0), True).reshape(24, 2, 8, 128)
    a, b = turn_columns(rows[:, 0], rows[:, 1], True)
    rows = jnp.stack([a, b], axis=1).reshape(384, 128)
    rows = lane_turn(rows, True).reshape(3, 4, 2, 2, 8, 128)
    for c in range(3):
        field = jnp.stack([rows[c, :, 0], rows[c, :, 1]], axis=2).reshape(16, 8, 128)
        v0[c] = fold_lanes(field).reshape(128, 128)

    for load in loads[2:]:
        load.wait()

    quad = tab[24]
    for x in range(8):
        at = pl.ds(2 * x, 2)
        xx, yy, zz, xy, xz, yz = (geo[k, at] for k in range(6))
        quad_x = quad * float(WF[x])
        weighted = quad_x * vis[at]
        det = (
            xx * (yy * zz - yz * yz) - xy * (xy * zz - yz * xz) + xz * (xy * yz - yy * xz)
        )
        mass_x = (HELM * quad_x) * det
        mass[at] = mass_x
        for k, g in enumerate((xx, yy, zz, xy, xz, yz)):
            gw[k, at] = weighted * g
        cross = (weighted * yz) * tab[25] + mass_x
        if x in (0, 7):
            end = float(ENDS[x])
            cross = cross + (weighted * xy) * (tab[26] * end) + (weighted * xz) * (tab[27] * end)
        zed[0, at] = cross
    local = (
        along_first(DS.T, gw[0])
        + along_second(tab, 16, gw[1])
        + along_third(mats[2], gw[2])
        + zed[0]
    )
    v0[3] = fold_lanes(local).reshape(128, 128)

    low_end = jnp.where(gx == 0, 1.0, 0.0)
    high_end = jnp.where(gx == n_gx - 1, 1.0, 0.0)
    marks = dirs[0].astype(jnp.float32) * low_end + dirs[1].astype(jnp.float32) * high_end
    v0[4] = jnp.zeros((128, 128), jnp.float32)
    v0[4, :48] = fold_lanes(marks.reshape(6, 8, 128)).reshape(48, 128)

    exchange(0, v0, N_FIRST, 4)

    low = jnp.full((8, 128), low_s[0], jnp.float32)
    high = jnp.full((8, 128), high_s[0], jnp.float32)
    middle, half = (high + low) * 0.5, (high - low) * 0.5
    ratio = middle / half
    damping = 1.0 / ratio
    factors = []
    for _ in range(2):
        following = 1.0 / (2.0 * ratio - damping)
        factors.append((following * damping, 2.0 * following / half))
        damping = following

    arrive(0, v0, 4)
    inverse = 1.0 / whole(0, v0, 3)
    inv[...] = inverse
    for c in range(3):
        flags = v0[4, pl.ds(16 * c, 16), :].reshape(2, 8, 128)
        free = jnp.where(flags > 0.5, 0.0, 1.0)
        keep_low = free * low_end + (1.0 - low_end)
        keep_high = free * high_end + (1.0 - high_end)
        scale[c, 0] = inverse[:2] * keep_low
        scale[c, 1] = inverse[14:] * keep_high

    def scaled(c, field):
        return jnp.concatenate(
            [scale[c, 0] * field[:2], inv[pl.ds(2, 12)] * field[2:14], scale[c, 1] * field[14:]],
            axis=0,
        )

    for c in range(3):
        start = scaled(c, whole(0, v0, c))
        zed[c] = start
        way[c] = start / middle
        out[c] = way[c].reshape(128, 128)

    for rnd, v in ((1, v1), (2, v2)):
        for c in range(3):
            field = way[c]
            slope1 = along_first(DF, field)
            slope2 = along_second(tab, 0, field)
            slope3 = along_third(mats[0], field)
            flux[0] = gw[0] * slope1 + gw[3] * slope2 + gw[4] * slope3
            flux[1] = gw[3] * slope1 + gw[1] * slope2 + gw[5] * slope3
            flux[2] = gw[4] * slope1 + gw[5] * slope2 + gw[2] * slope3
            image = (
                along_first(DF.T, flux[0])
                + along_second(tab, 8, flux[1])
                + along_third(mats[1], flux[2])
                + mass[...] * field
            )
            v[c] = fold_lanes(image).reshape(128, 128)
        exchange(rnd, v, 3, 3)
        arrive(rnd, v, 3)
        keep_by, add_by = factors[rnd - 1]
        for c in range(3):
            rest = zed[c] - scaled(c, whole(rnd, v, c))
            zed[c] = rest
            step = keep_by * way[c] + add_by * rest
            way[c] = step
            out[c] = out[c] + step.reshape(128, 128)

    for rnd, v, fields, x_fields in ((0, v0, N_FIRST, 4), (1, v1, 3, 3), (2, v2, 3, 3)):
        for side, (step_y, step_z) in enumerate(SIDES):

            @pl.when(inside(step_y, step_z))
            def _():
                side_copy(rnd, side, fields)(True).wait_send()

        for side, step in enumerate((-1, 1)):

            @pl.when((gx + step >= 0) & (gx + step < n_gx))
            def _():
                first_copy(rnd, v, side, x_fields, True).wait_send()


def to_slots(field, slot, out):
    rows = field[...].reshape(3, 4, 2, 2, 8, 128)
    rows = jnp.stack([rows[:, :, 0], rows[:, :, 1]], axis=3).reshape(384, 128)
    rows = lane_turn(rows, False).reshape(24, 2, 8, 128)
    a, b = turn_columns(rows[:, 0], rows[:, 1], False)
    rows = lane_turn(jnp.stack([a, b], axis=1).reshape(384, 128), False).reshape(3, 4, 32, 128)
    one_hot = slot_matrix(slot[...]).T.astype(jnp.bfloat16)
    pair = jnp.concatenate([one_hot, one_hot], axis=1)
    for c in range(3):
        wide = jnp.concatenate([rows[c, ip] for ip in range(4)], axis=1)
        high, low = halves(wide)
        out[c] = jnp.dot(
            pair, jnp.concatenate([high, low], axis=0), preferred_element_type=jnp.float32
        )


def shards(sizes, right_side, geometry, viscosity, eig_low, eig_high, element_slot, dirichlet):
    f32 = jnp.float32
    anywhere = pl.BlockSpec(memory_space=pl.ANY)
    scalar = pl.BlockSpec(memory_space=pltpu.SMEM)
    vmem = pl.BlockSpec(memory_space=pltpu.VMEM)
    field = pl.pallas_call(
        functools.partial(kernel, sizes),
        out_shape=jax.ShapeDtypeStruct((3, 128, 128), f32),
        in_specs=[anywhere] * 3 + [scalar] * 2 + [anywhere] * 4,
        out_specs=vmem,
        scratch_shapes=[
            pltpu.VMEM((3, 32, 512), f32),
            pltpu.VMEM((6, 16, 8, 128), f32),
            pltpu.VMEM((16, 8, 128), f32),
            pltpu.VMEM((1, 32), jnp.int32),
            pltpu.VMEM((2, 3, 16, 128), jnp.int32),
            pltpu.VMEM((28, 8, 128), f32),
            pltpu.VMEM((3, 256, 256), jnp.bfloat16),
            pltpu.VMEM((6, 16, 8, 128), f32),
            pltpu.VMEM((16, 8, 128), f32),
            pltpu.VMEM((16, 8, 128), f32),
            pltpu.VMEM((3, 2, 2, 8, 128), f32),
            pltpu.VMEM((3, 16, 8, 128), f32),
            pltpu.VMEM((3, 16, 8, 128), f32),
            pltpu.VMEM((3, 16, 8, 128), f32),
            pltpu.VMEM((5, 128, 128), f32),
            pltpu.VMEM((3, 128, 128), f32),
            pltpu.VMEM((3, 128, 128), f32),
            pltpu.VMEM((3, 2, 5, 8, 128), f32),
            pltpu.VMEM((3, 2, 8, 128), f32),
            pltpu.VMEM((3, 2, 5, 8, 128), f32),
            pltpu.VMEM((3, 6, 2, 8, 128), f32),
            pltpu.VMEM((3, 2, 4, 16, 128), f32),
            pltpu.SemaphoreType.DMA((7,)),
            pltpu.SemaphoreType.DMA((3, 2)),
            pltpu.SemaphoreType.DMA((3, 2)),
            pltpu.SemaphoreType.DMA((3, 6)),
            pltpu.SemaphoreType.DMA((3, 6)),
            pltpu.SemaphoreType.DMA((3, 2)),
            pltpu.SemaphoreType.DMA((3, 2)),
        ],
        compiler_params=pltpu.CompilerParams(collective_id=0, has_side_effects=True),
        name="solve",
    )(
        jnp.swapaxes(right_side, 1, 2),
        geometry.reshape(6, 16, 8, 128),
        viscosity.reshape(16, 8, 128),
        eig_low,
        eig_high,
        element_slot,
        dirichlet,
        jnp.asarray(lane_table()),
        jnp.asarray(lane_matrices()),
    )
    slots = pl.pallas_call(
        to_slots,
        out_shape=jax.ShapeDtypeStruct((3, 32, 512), f32),
        in_specs=[vmem, vmem],
        out_specs=vmem,
        name="to_slots",
    )(field.reshape(3, 16, 8, 128), element_slot)
    return jnp.swapaxes(slots, 1, 2)


def solution(mesh):
    sizes = tuple(mesh.shape[axis] for axis in ("gx", "gy", "gz"))
    return jax.shard_map(
        functools.partial(shards, sizes),
        mesh=mesh,
        in_specs=(
            P(None, None, ("gx", "gy", "gz")),
            P(None, "gx", "gy", "gz"),
            P("gx", "gy", "gz"),
            P(),
            P(),
            P(("gx", "gy", "gz"), None),
            P(None, None, "gy", "gz"),
        ),
        out_specs=P(None, None, ("gx", "gy", "gz")),
        check_vma=False,
    )
```

time: 156 us -> 51.8 us (0.33)
  the two profiles are of different devices: /device:TPU:55 before, /device:TPU:31 now
where the time goes in v1:
time: 51.8 us; the launch traced here: 51.6 us
  Pallas kernels  50.3 us (97%)
  between operations  1.3 us (3%)
    pallas_call x1, Pallas kernels, shards(): pl.pallas_call(functools.partial(kernel, sizes), out_shape=jax.ShapeDtype...  48.3 us
    pallas_call x1, Pallas kernels, shards(): pl.pallas_call(to_slots, out_shape=jax.ShapeDtypeStruct((3, 32, 512), f32...  1.97 us

profile of v1, /device:TPU:31, one launch (start us, length us, event | category | flops | bytes accessed | tf_op | source)
XLA Modules:
  0.0 51.6 jit_solution(17061760244244785641)
XLA Ops:
  1.3 48.3 %solve.1 = f32[3,128,128]{2,1,0:T(8,128)} custom-call(f32[3,32,512]{2,1,0:T(8,128)} %bitcast.7, f32[6,16,8,128]{3,2,1,0:T(8,128)} %bitcast.6, f32[16,8,128]{2,1,0:T(8,128)} %bitcast.8, f32[1]{0:T(128)S(6)} %copy.10.low_s, f32[1]{0:T(128)S(6)} %copy.11.high_s, s32[1,32]{1,0:T(1,128)} %slot.1, s32[2,3,16,128]{3,2,1,0:T(8,128)} %dir_h.1, ...), custom_call_target="tpu_custom_call" | custom-call | tf_op jit(solution)/shard_map/solve/pallas_call | solution.py:507
  49.6 2.0 %to_slots.1 = f32[3,32,512]{2,1,0:T(8,128)} custom-call(f32[3,16,8,128]{3,2,1,0:T(8,128)} %bitcast.5, s32[1,32]{1,0:T(1,128)} %slot.1), custom_call_target="tpu_custom_call" | custom-call | tf_op jit(solution)/shard_map/to_slots/pallas_call | solution.py:556

commit v2 on v1

--- a/solution.py
+++ b/solution.py
@@ -93,41 +93,42 @@
 
 
 def turn_columns(a, b, down):
-    sub = lax.broadcasted_iota(jnp.int32, a.shape, 1)
-    group = lax.broadcasted_iota(jnp.int32, a.shape, 2) // 8
-    for bit in (1, 2, 4):
-        here = (group & bit) != 0
-        if down:
-            ra, rb = pltpu.roll(a, bit, 1), pltpu.roll(b, bit, 1)
-            na, nb = jnp.where(sub < bit, rb, ra), jnp.where(sub < bit, ra, rb)
-        else:
-            ra, rb = pltpu.roll(a, 8 - bit, 1), pltpu.roll(b, 8 - bit, 1)
-            na, nb = jnp.where(sub < 8 - bit, ra, rb), jnp.where(sub < 8 - bit, rb, ra)
-        a, b = jnp.where(here, na, a), jnp.where(here, nb, b)
-    here = (group & 8) != 0
-    return jnp.where(here, b, a), jnp.where(here, a, b)
+    sub = lax.broadcasted_iota(jnp.int32, (8, 128), 0)
+    group = lax.broadcasted_iota(jnp.int32, (8, 128), 1) // 8
+    start = (sub - group if down else sub + group) & 15
+    straight = start < 8
+    low, high = [], []
+    for n in range(a.shape[0]):
+        ta = jnp.take_along_axis(a[n], start & 7, axis=0, mode="promise_in_bounds")
+        tb = jnp.take_along_axis(b[n], start & 7, axis=0, mode="promise_in_bounds")
+        low.append(jnp.where(straight, ta, tb))
+        high.append(jnp.where(straight, tb, ta))
+    return jnp.stack(low), jnp.stack(high)
 
 
 def lane_turn(x, left):
     if not left:
         return pltpu.roll(x, 0, 1, stride=8, stride_axis=0)
     row = lax.broadcasted_iota(jnp.int32, x.shape, 0)
-    for bit in (1, 2, 4, 8):
-        x = jnp.where((row & bit) != 0, pltpu.roll(x, 128 - 8 * bit, 1), x)
-    return x
-
-
-def along_first(matrix, field):
-    planes = [field[2 * i : 2 * i + 2] for i in range(8)]
+    lane = lax.broadcasted_iota(jnp.int32, x.shape, 1)
+    source = (lane + 8 * (row & 15)) & 127
+    return jnp.take_along_axis(x, source, axis=1, mode="promise_in_bounds")
+
+
+def along_first(matrix, planes, outs=range(8)):
     out = []
-    for a in range(8):
+    for a in outs:
         total = None
-        for i in range(8):
+        for i, plane in planes.items():
             if abs(matrix[a, i]) > 0:
-                term = planes[i] * float(matrix[a, i])
+                term = plane * float(matrix[a, i])
                 total = term if total is None else total + term
         out.append(total)
     return jnp.concatenate(out, axis=0)
+
+
+def planes_of(field, first=0):
+    return {first + i: field[2 * i : 2 * i + 2] for i in range(field.shape[0] // 2)}
 
 
 def along_second(tab, base, field):
@@ -138,11 +139,11 @@
 
 
 def along_third(matrix, field):
-    high, low = halves(field.reshape(128, 128))
+    high, low = halves(field.reshape(-1, 128))
     both = jnp.dot(
         jnp.concatenate([high, low], axis=1), matrix, preferred_element_type=jnp.float32
     )
-    return (both[:, :128] + both[:, 128:]).reshape(16, 8, 128)
+    return (both[:, :128] + both[:, 128:]).reshape(field.shape)
 
 
 def fold_lanes(field):
@@ -159,8 +160,8 @@
 def kernel(
     sizes,
     rs_h, geo_h, vis_h, low_s, high_s, slot_h, dir_h, tab_h, mat_h,
-    out,
-    rs, geo, vis, slot, dirs, tab, mats, gw, mass, inv, scale, zed, way, flux,
+    out, place,
+    rs, geo, vis, slot, dirs, tab, mats, gw, mass, inv, scale, zed, way, flux, edge, total,
     v0, v1, v2, ysend, zsend, yrecv, zrecv, xrecv,
     in_sem, ysem, yrsem, zsem, zrsem, xsem, xrsem,
 ):
@@ -281,15 +282,21 @@
             v[f, pl.ds(8, 8, stride=16), :] = row7 + row8
             ysend[rnd, 0, f] = v[f, pl.ds(0, 8, stride=16), :]
             ysend[rnd, 1, f] = v[f, pl.ds(15, 8, stride=16), :]
+        if rnd == 0:
+            pl.semaphore_wait(barrier, count)
+        for side in (0, 1):
+
+            @pl.when(inside(*SIDES[side]))
+            def _():
+                side_copy(rnd, side, fields)(True).start()
+
         groups = []
         for n, group, tile in packed(v, fields):
             zsend[rnd, n] = tile
             groups.append(group)
-        if rnd == 0:
-            pl.semaphore_wait(barrier, count)
-        for side, (step_y, step_z) in enumerate(SIDES):
-
-            @pl.when(inside(step_y, step_z))
+        for side in (4, 5, 6, 7, 2, 3):
+
+            @pl.when(inside(*SIDES[side]))
             def _():
                 side_copy(rnd, side, fields)(True).start()
 
@@ -307,6 +314,11 @@
         def swapped(minus, plus):
             return jnp.where(odd, pltpu.roll(minus, 1, 1), pltpu.roll(plus, 127, 1))
 
+        for f in range(fields):
+            for side, row in ((0, 0), (1, 15)):
+                rows = pl.ds(row, 8, stride=16)
+                v[f, rows, :] = v[f, rows, :] + yrecv[rnd, side, f]
+        nears = []
         for n, group in enumerate(groups):
             near = swapped(zrecv[rnd, 0, n], zrecv[rnd, 1, n])
             below = swapped(zrecv[rnd, 2, n], zrecv[rnd, 3, n])
@@ -315,22 +327,25 @@
             above = pltpu.roll(pltpu.roll(above, 7, 0), 2, 1)
             upper_tile = (lane // 2) % 2 == 1
             near = near + jnp.where((sub == 0) & ~upper_tile, below, 0.0)
-            near = near + jnp.where((sub == 7) & upper_tile, above, 0.0)
-            order = sorted(range(len(group)), key=lambda q: group[q][1] not in (0, 1, 14, 15))
-            for q in order:
-                f, t = group[q]
-                moved = pltpu.roll(near, (128 - (2 * q + 1)) % 128, 1)
-                v[f, pl.ds(8 * t, 8), :] = v[f, pl.ds(8 * t, 8), :] + jnp.where(rim, moved, 0.0)
-        for f in range(fields):
-            for side, row in ((0, 0), (1, 15)):
-                rows = pl.ds(row, 8, stride=16)
-                v[f, rows, :] = v[f, rows, :] + yrecv[rnd, side, f]
+            nears.append(near + jnp.where((sub == 7) & upper_tile, above, 0.0))
+
+        def unpack(wanted):
+            for near, group in zip(nears, groups):
+                for q, (f, t) in enumerate(group):
+                    if (t in (0, 1, 14, 15) and f < 4) == wanted:
+                        moved = pltpu.roll(near, (128 - (2 * q + 1)) % 128, 1)
+                        tile = pl.ds(8 * t, 8)
+                        v[f, tile, :] = v[f, tile, :] + jnp.where(rim, moved, 0.0)
+
+        unpack(True)
         for side, step in enumerate((-1, 1)):
 
             @pl.when((gx + step >= 0) & (gx + step < n_gx))
             def _():
                 first_copy(rnd, v, side, x_fields, True).start()
 
+        unpack(False)
+
     def arrive(rnd, v, x_fields):
         for side, step in enumerate((-1, 1)):
 
@@ -338,23 +353,66 @@
             def _():
                 first_copy(rnd, v, side, x_fields, False).wait_recv()
 
-    def field_of(v, f):
-        return v[f].reshape(16, 8, 128)
-
-    def whole(rnd, v, f):
-        own = field_of(v, f)
-        return jnp.concatenate(
-            [
-                own[:2] + xrecv[rnd, 0, f].reshape(2, 8, 128),
-                own[2:14],
-                own[14:] + xrecv[rnd, 1, f].reshape(2, 8, 128),
-            ],
-            axis=0,
+    inner = pl.ds(2, 12)
+
+    def middle_of(v, f):
+        return v[f, pl.ds(16, 96), :].reshape(12, 8, 128)
+
+    def rims_of(rnd, v, f):
+        first = v[f, pl.ds(0, 16), :] + xrecv[rnd, 0, f]
+        last = v[f, pl.ds(112, 16), :] + xrecv[rnd, 1, f]
+        return jnp.concatenate([first.reshape(2, 8, 128), last.reshape(2, 8, 128)], axis=0)
+
+    def put_rims(ref, c, value):
+        ref[c, pl.ds(0, 2)] = value[:2]
+        ref[c, pl.ds(14, 2)] = value[2:]
+
+    def get_rims(ref, c):
+        return jnp.concatenate([ref[c, pl.ds(0, 2)], ref[c, pl.ds(14, 2)]], axis=0)
+
+    def fluxes(c, where, slopes, base=None):
+        s1, s2, s3 = slopes
+        for k, (a, b, d) in enumerate(((0, 3, 4), (3, 1, 5), (4, 5, 2))):
+            flux[c, k, where] = gw[a, where] * s1 + gw[b, where] * s2 + gw[d, where] * s3
+
+    def ahead(c):
+        field = way[c, inner]
+        planes = planes_of(field, 1)
+        edge[c] = along_first(DF, planes, (0, 7))
+        fluxes(
+            c,
+            inner,
+            (
+                along_first(DF, planes, range(1, 7)),
+                along_second(tab, 0, field),
+                along_third(mats[0], field),
+            ),
+        )
+
+    def image_of(c):
+        rims = get_rims(way, c)
+        ends = {0: rims[:2], 7: rims[2:]}
+        s1 = edge[c] + along_first(DF, ends, (0, 7))
+        s2 = along_second(tab, 0, rims)
+        s3 = along_third(mats[0], rims)
+        for n, where in enumerate((pl.ds(0, 2), pl.ds(14, 2))):
+            part = slice(2 * n, 2 * n + 2)
+            fluxes(c, where, (s1[part], s2[part], s3[part]))
+        more = along_first(DF, ends, range(1, 7))
+        for k, a in enumerate((0, 3, 4)):
+            flux[c, k, inner] = flux[c, k, inner] + gw[a, inner] * more
+        return (
+            along_first(DF.T, planes_of(flux[c, 0]))
+            + along_second(tab, 8, flux[c, 1])
+            + along_third(mats[1], flux[c, 2])
+            + mass[...] * way[c]
         )
 
     loads[0].wait()
     loads[1].wait()
-    one_hot = slot_matrix(slot[...]).astype(jnp.bfloat16)
+    one_hot = slot_matrix(slot[...])
+    place[...] = one_hot.T
+    one_hot = one_hot.astype(jnp.bfloat16)
     pair = jnp.concatenate([one_hot, one_hot], axis=1)
     blocks = []
     for c in range(3):
@@ -394,7 +452,7 @@
             cross = cross + (weighted * xy) * (tab[26] * end) + (weighted * xz) * (tab[27] * end)
         zed[0, at] = cross
     local = (
-        along_first(DS.T, gw[0])
+        along_first(DS.T, planes_of(gw[0]))
         + along_second(tab, 16, gw[1])
         + along_third(mats[2], gw[2])
         + zed[0]
@@ -420,54 +478,55 @@
         factors.append((following * damping, 2.0 * following / half))
         damping = following
 
+    inverse = 1.0 / middle_of(v0, 3)
+    inv[inner] = inverse
+    for c in range(3):
+        start = inverse * middle_of(v0, c)
+        zed[c, inner] = start
+        way[c, inner] = start / middle
+        out[c, pl.ds(16, 96), :] = way[c, inner].reshape(96, 128)
+    for c in range(3):
+        ahead(c)
     arrive(0, v0, 4)
-    inverse = 1.0 / whole(0, v0, 3)
-    inv[...] = inverse
+    inverse = 1.0 / rims_of(0, v0, 3)
     for c in range(3):
         flags = v0[4, pl.ds(16 * c, 16), :].reshape(2, 8, 128)
         free = jnp.where(flags > 0.5, 0.0, 1.0)
         keep_low = free * low_end + (1.0 - low_end)
         keep_high = free * high_end + (1.0 - high_end)
-        scale[c, 0] = inverse[:2] * keep_low
-        scale[c, 1] = inverse[14:] * keep_high
-
-    def scaled(c, field):
-        return jnp.concatenate(
-            [scale[c, 0] * field[:2], inv[pl.ds(2, 12)] * field[2:14], scale[c, 1] * field[14:]],
-            axis=0,
-        )
-
-    for c in range(3):
-        start = scaled(c, whole(0, v0, c))
-        zed[c] = start
-        way[c] = start / middle
-        out[c] = way[c].reshape(128, 128)
+        scale[c] = inverse * jnp.concatenate([keep_low, keep_high], axis=0)
+        start = scale[c] * rims_of(0, v0, c)
+        put_rims(zed, c, start)
+        put_rims(way, c, start / middle)
 
     for rnd, v in ((1, v1), (2, v2)):
         for c in range(3):
-            field = way[c]
-            slope1 = along_first(DF, field)
-            slope2 = along_second(tab, 0, field)
-            slope3 = along_third(mats[0], field)
-            flux[0] = gw[0] * slope1 + gw[3] * slope2 + gw[4] * slope3
-            flux[1] = gw[3] * slope1 + gw[1] * slope2 + gw[5] * slope3
-            flux[2] = gw[4] * slope1 + gw[5] * slope2 + gw[2] * slope3
-            image = (
-                along_first(DF.T, flux[0])
-                + along_second(tab, 8, flux[1])
-                + along_third(mats[1], flux[2])
-                + mass[...] * field
-            )
-            v[c] = fold_lanes(image).reshape(128, 128)
+            v[c] = fold_lanes(image_of(c)).reshape(128, 128)
         exchange(rnd, v, 3, 3)
-        arrive(rnd, v, 3)
         keep_by, add_by = factors[rnd - 1]
         for c in range(3):
-            rest = zed[c] - scaled(c, whole(rnd, v, c))
-            zed[c] = rest
-            step = keep_by * way[c] + add_by * rest
-            way[c] = step
-            out[c] = out[c] + step.reshape(128, 128)
+            rest = zed[c, inner] - inv[inner] * middle_of(v, c)
+            step = keep_by * way[c, inner] + add_by * rest
+            out[c, pl.ds(16, 96), :] = out[c, pl.ds(16, 96), :] + step.reshape(96, 128)
+            if rnd == 1:
+                zed[c, inner] = rest
+                way[c, inner] = step
+        for c in range(3):
+            if rnd == 1:
+                ahead(c)
+                total[c] = get_rims(way, c)
+        arrive(rnd, v, 3)
+        for c in range(3):
+            rest = get_rims(zed, c) - scale[c] * rims_of(rnd, v, c)
+            step = keep_by * get_rims(way, c) + add_by * rest
+            if rnd == 1:
+                put_rims(zed, c, rest)
+                put_rims(way, c, step)
+            total[c] = total[c] + step
+            if rnd == 2:
+                whole = total[c].reshape(32, 128)
+                out[c, pl.ds(0, 16), :] = whole[:16]
+                out[c, pl.ds(112, 16), :] = whole[16:]
 
     for rnd, v, fields, x_fields in ((0, v0, N_FIRST, 4), (1, v1, 3, 3), (2, v2, 3, 3)):
         for side, (step_y, step_z) in enumerate(SIDES):
@@ -483,13 +542,13 @@
                 first_copy(rnd, v, side, x_fields, True).wait_send()
 
 
-def to_slots(field, slot, out):
+def to_slots(field, place, out):
     rows = field[...].reshape(3, 4, 2, 2, 8, 128)
     rows = jnp.stack([rows[:, :, 0], rows[:, :, 1]], axis=3).reshape(384, 128)
     rows = lane_turn(rows, False).reshape(24, 2, 8, 128)
     a, b = turn_columns(rows[:, 0], rows[:, 1], False)
     rows = lane_turn(jnp.stack([a, b], axis=1).reshape(384, 128), False).reshape(3, 4, 32, 128)
-    one_hot = slot_matrix(slot[...]).T.astype(jnp.bfloat16)
+    one_hot = place[...].astype(jnp.bfloat16)
     pair = jnp.concatenate([one_hot, one_hot], axis=1)
     for c in range(3):
         wide = jnp.concatenate([rows[c, ip] for ip in range(4)], axis=1)
@@ -504,11 +563,11 @@
     anywhere = pl.BlockSpec(memory_space=pl.ANY)
     scalar = pl.BlockSpec(memory_space=pltpu.SMEM)
     vmem = pl.BlockSpec(memory_space=pltpu.VMEM)
-    field = pl.pallas_call(
+    field, place = pl.pallas_call(
         functools.partial(kernel, sizes),
-        out_shape=jax.ShapeDtypeStruct((3, 128, 128), f32),
+        out_shape=(pltpu.VMEM((3, 128, 128), f32), pltpu.VMEM((32, 32), f32)),
         in_specs=[anywhere] * 3 + [scalar] * 2 + [anywhere] * 4,
-        out_specs=vmem,
+        out_specs=(vmem, vmem),
         scratch_shapes=[
             pltpu.VMEM((3, 32, 512), f32),
             pltpu.VMEM((6, 16, 8, 128), f32),
@@ -520,10 +579,12 @@
             pltpu.VMEM((6, 16, 8, 128), f32),
             pltpu.VMEM((16, 8, 128), f32),
             pltpu.VMEM((16, 8, 128), f32),
-            pltpu.VMEM((3, 2, 2, 8, 128), f32),
+            pltpu.VMEM((3, 4, 8, 128), f32),
             pltpu.VMEM((3, 16, 8, 128), f32),
             pltpu.VMEM((3, 16, 8, 128), f32),
-            pltpu.VMEM((3, 16, 8, 128), f32),
+            pltpu.VMEM((3, 3, 16, 8, 128), f32),
+            pltpu.VMEM((3, 4, 8, 128), f32),
+            pltpu.VMEM((3, 4, 8, 128), f32),
             pltpu.VMEM((5, 128, 128), f32),
             pltpu.VMEM((3, 128, 128), f32),
             pltpu.VMEM((3, 128, 128), f32),
@@ -558,8 +619,8 @@
         out_shape=jax.ShapeDtypeStruct((3, 32, 512), f32),
         in_specs=[vmem, vmem],
         out_specs=vmem,
-        name="to_slots",
-    )(field.reshape(3, 16, 8, 128), element_slot)
+        name="to_slots", compiler_params=pltpu.CompilerParams(vmem_limit_bytes=8 << 20),
+    )(field.reshape(3, 16, 8, 128), place)
     return jnp.swapaxes(slots, 1, 2)
 
 

time: 51.8 us -> 49 us (0.946)
  Pallas kernels: 50.3 us -> 47.6 us
    pallas_call x1, Pallas kernels: 48.3 us -> 46.6 us  [shards(): pl.pallas_call(functools.partial(kernel, sizes), out_shape=(pltpu.VMEM((3...]
    pallas_call x1, Pallas kernels: 1.97 us -> 1 us  [shards(): pl.pallas_call(to_slots, out_shape=jax.ShapeDtypeStruct((3, 32, 512), f32...]
where the time goes in v2:
time: 49 us; the launch traced here: 48.9 us
  Pallas kernels  47.6 us (97%)
  between operations  1.3 us (3%)
    pallas_call x1, Pallas kernels, shards(): pl.pallas_call(functools.partial(kernel, sizes), out_shape=(pltpu.VMEM((3...  46.6 us
    pallas_call x1, Pallas kernels, shards(): pl.pallas_call(to_slots, out_shape=jax.ShapeDtypeStruct((3, 32, 512), f32...  1 us

profile of v2, /device:TPU:31, one launch (start us, length us, event | category | flops | bytes accessed | tf_op | source)
XLA Modules:
  0.0 48.9 jit_solution(15000009471177962380)
XLA Ops:
  1.3 46.6 %solve.1 = (f32[3,128,128]{2,1,0:T(8,128)S(1)}, f32[32,32]{1,0:T(8,128)S(1)}) custom-call(f32[3,32,512]{2,1,0:T(8,128)} %bitcast.7, f32[6,16,8,128]{3,2,1,0:T(8,128)} %bitcast.6, f32[16,8,128]{2,1,0:T(8,128)} %bitcast.8, f32[1]{0:T(128)S(6)} %copy.10.low_s, f32[1]{0:T(128)S(6)} %copy.11.high_s, s32[1,32]{1,0:T(1,128)} %slot_h.1, s32[2,3,16,128]{3,2,1,0:T(8,128)} %dir_h.1, ...), custom_call_target="tpu_custom_call" | custom-call | tf_op jit(solution)/shard_map/solve/pallas_call | solution.py:566
  47.9 1.0 %to_slots.1 = f32[3,32,512]{2,1,0:T(8,128)} custom-call(f32[3,16,8,128]{3,2,1,0:T(8,128)S(1)} %bitcast.5, f32[32,32]{1,0:T(8,128)S(1)} %get-tuple-element.8.place), custom_call_target="tpu_custom_call" | custom-call | tf_op jit(solution)/shard_map/to_slots/pallas_call | solution.py:617

commit v3 on v2

--- a/solution.py
+++ b/solution.py
@@ -125,6 +125,25 @@
                 total = term if total is None else total + term
         out.append(total)
     return jnp.concatenate(out, axis=0)
+
+
+def mirrored(matrix, sign, field):
+    wide = np.asarray(matrix, np.float64)
+    planes = planes_of(field)
+    even = [planes[i] + planes[7 - i] for i in range(4)]
+    odd = [planes[i] - planes[7 - i] for i in range(4)]
+    first, last = [], []
+    for a in range(4):
+        parts = []
+        for terms, flip in ((even, 1.0), (odd, -1.0)):
+            total = None
+            for i in range(4):
+                term = terms[i] * float(0.5 * (wide[a, i] + flip * wide[a, 7 - i]))
+                total = term if total is None else total + term
+            parts.append(total)
+        first.append(parts[0] + parts[1])
+        last.append((parts[0] - parts[1]) if sign > 0 else (parts[1] - parts[0]))
+    return jnp.concatenate(first + last[::-1], axis=0)
 
 
 def planes_of(field, first=0):
@@ -402,14 +421,14 @@
         for k, a in enumerate((0, 3, 4)):
             flux[c, k, inner] = flux[c, k, inner] + gw[a, inner] * more
         return (
-            along_first(DF.T, planes_of(flux[c, 0]))
+            mirrored(DF.T, -1, flux[c, 0])
             + along_second(tab, 8, flux[c, 1])
             + along_third(mats[1], flux[c, 2])
             + mass[...] * way[c]
         )
 
-    loads[0].wait()
-    loads[1].wait()
+    for load in loads:
+        load.wait()
     one_hot = slot_matrix(slot[...])
     place[...] = one_hot.T
     one_hot = one_hot.astype(jnp.bfloat16)
@@ -429,9 +448,6 @@
     for c in range(3):
         field = jnp.stack([rows[c, :, 0], rows[c, :, 1]], axis=2).reshape(16, 8, 128)
         v0[c] = fold_lanes(field).reshape(128, 128)
-
-    for load in loads[2:]:
-        load.wait()
 
     quad = tab[24]
     for x in range(8):
@@ -452,7 +468,7 @@
             cross = cross + (weighted * xy) * (tab[26] * end) + (weighted * xz) * (tab[27] * end)
         zed[0, at] = cross
     local = (
-        along_first(DS.T, planes_of(gw[0]))
+        mirrored(DS.T, 1, gw[0])
         + along_second(tab, 16, gw[1])
         + along_third(mats[2], gw[2])
         + zed[0]

time: 49 us -> 49 us (level)
  no operation moved by 1% of the time
where the time goes in v3:
time: 49 us; the launch traced here: 48.8 us
  Pallas kernels  47.5 us (97%)
  between operations  1.3 us (3%)
    pallas_call x1, Pallas kernels, shards(): pl.pallas_call(functools.partial(kernel, sizes), out_shape=(pltpu.VMEM((3...  46.5 us
    pallas_call x1, Pallas kernels, shards(): pl.pallas_call(to_slots, out_shape=jax.ShapeDtypeStruct((3, 32, 512), f32...  1 us

profile of v3, /device:TPU:31, one launch (start us, length us, event | category | flops | bytes accessed | tf_op | source)
XLA Modules:
  0.0 48.8 jit_solution(4955235277878167072)
XLA Ops:
  1.3 46.5 %solve.1 = (f32[3,128,128]{2,1,0:T(8,128)S(1)}, f32[32,32]{1,0:T(8,128)S(1)}) custom-call(f32[3,32,512]{2,1,0:T(8,128)} %bitcast.7, f32[6,16,8,128]{3,2,1,0:T(8,128)} %bitcast.6, f32[16,8,128]{2,1,0:T(8,128)} %bitcast.8, f32[1]{0:T(128)S(6)} %copy.10.low_s, f32[1]{0:T(128)S(6)} %copy.11.high_s, s32[1,32]{1,0:T(1,128)} %slot_h.1, s32[2,3,16,128]{3,2,1,0:T(8,128)} %dir_h.1, ...), custom_call_target="tpu_custom_call" | custom-call | tf_op jit(solution)/shard_map/solve/pallas_call | solution.py:582
  47.8 1.0 %to_slots.1 = f32[3,32,512]{2,1,0:T(8,128)} custom-call(f32[3,16,8,128]{3,2,1,0:T(8,128)S(1)} %bitcast.5, f32[32,32]{1,0:T(8,128)S(1)} %get-tuple-element.8.place), custom_call_target="tpu_custom_call" | custom-call | tf_op jit(solution)/shard_map/to_slots/pallas_call | solution.py:633

commit v4 on v2

--- a/solution.py
+++ b/solution.py
@@ -46,6 +46,8 @@
     return (weights, derivative)
 
 
+ENDS_AT = (0, 1, 14, 15)
+
 WEIGHTS, DERIVATIVE = gll_tables(DEGREE)
 DF = DERIVATIVE.astype(np.float32)
 WF = WEIGHTS.astype(np.float32)
@@ -162,8 +164,8 @@
     rs_h, geo_h, vis_h, low_s, high_s, slot_h, dir_h, tab_h, mat_h,
     out, place,
     rs, geo, vis, slot, dirs, tab, mats, gw, mass, inv, scale, zed, way, flux, edge, total,
-    v0, v1, v2, ysend, zsend, yrecv, zrecv, xrecv,
-    in_sem, ysem, yrsem, zsem, zrsem, xsem, xrsem,
+    v0, v1, v2, own, fsend, frecv, ysend, zsend, yrecv, zrecv, xrecv,
+    in_sem, ysem, yrsem, zsem, zrsem, xsem, xrsem, fsem, frsem,
 ):
     n_gx, n_gy, n_gz = sizes
     gx, gy, gz = lax.axis_index("gx"), lax.axis_index("gy"), lax.axis_index("gz")
@@ -199,6 +201,8 @@
     yrecv[...] = jnp.zeros_like(yrecv)
     zrecv[...] = jnp.zeros_like(zrecv)
     xrecv[...] = jnp.zeros_like(xrecv)
+    frecv[...] = jnp.zeros_like(frecv)
+    fsend[...] = jnp.zeros_like(fsend)
 
     barrier = pltpu.get_barrier_semaphore()
     count = 0
@@ -260,6 +264,20 @@
             device_id_type=MESH,
         )
 
+    def fix_copy(rnd, side, tiles, to):
+        step = (-1, 1)[side]
+        return pltpu.make_async_remote_copy(
+            src_ref=fsend.at[rnd, side, pl.ds(0, tiles)],
+            dst_ref=frecv.at[rnd, (1 - side) if to else side, pl.ds(0, tiles)],
+            send_sem=fsem.at[rnd, side],
+            recv_sem=frsem.at[rnd, (1 - side) if to else side],
+            device_id={"gx": gx + step, "gy": gy, "gz": gz},
+            device_id_type=MESH,
+        )
+
+    def beside(side):
+        return (gx + (-1, 1)[side] >= 0) & (gx + (-1, 1)[side] < n_gx)
+
     def packed(v, fields):
         lane = lax.broadcasted_iota(jnp.int32, (8, 128), 1) // 2
         groups = [[(f, t) for f in range(3) for t in range(16)]]
@@ -300,6 +318,12 @@
             def _():
                 side_copy(rnd, side, fields)(True).start()
 
+        for side in (0, 1):
+
+            @pl.when(beside(side))
+            def _():
+                first_copy(rnd, v, side, x_fields, True).start()
+
         for side, (step_y, step_z) in enumerate(SIDES):
 
             @pl.when(inside(step_y, step_z))
@@ -314,10 +338,6 @@
         def swapped(minus, plus):
             return jnp.where(odd, pltpu.roll(minus, 1, 1), pltpu.roll(plus, 127, 1))
 
-        for f in range(fields):
-            for side, row in ((0, 0), (1, 15)):
-                rows = pl.ds(row, 8, stride=16)
-                v[f, rows, :] = v[f, rows, :] + yrecv[rnd, side, f]
         nears = []
         for n, group in enumerate(groups):
             near = swapped(zrecv[rnd, 0, n], zrecv[rnd, 1, n])
@@ -329,29 +349,47 @@
             near = near + jnp.where((sub == 0) & ~upper_tile, below, 0.0)
             nears.append(near + jnp.where((sub == 7) & upper_tile, above, 0.0))
 
-        def unpack(wanted):
-            for near, group in zip(nears, groups):
-                for q, (f, t) in enumerate(group):
-                    if (t in (0, 1, 14, 15) and f < 4) == wanted:
-                        moved = pltpu.roll(near, (128 - (2 * q + 1)) % 128, 1)
-                        tile = pl.ds(8 * t, 8)
-                        v[f, tile, :] = v[f, tile, :] + jnp.where(rim, moved, 0.0)
-
-        unpack(True)
-        for side, step in enumerate((-1, 1)):
-
-            @pl.when((gx + step >= 0) & (gx + step < n_gx))
+        tiles = len(groups) + 1
+        for side in (0, 1):
+            for n, near in enumerate(nears):
+                fsend[rnd, side, n] = near
+            for f in range(x_fields):
+                for y_side in (0, 1):
+                    fsend[rnd, side, tiles - 1, pl.ds(2 * f + y_side, 1), :] = yrecv[
+                        rnd, y_side, f, pl.ds(7 * side, 1), :
+                    ]
+
+            @pl.when(beside(side))
             def _():
-                first_copy(rnd, v, side, x_fields, True).start()
-
-        unpack(False)
+                fix_copy(rnd, side, tiles, True).start()
+
+        for near, group in zip(nears, groups):
+            for q, (f, t) in enumerate(group):
+                added = jnp.where(rim, pltpu.roll(near, (128 - (2 * q + 1)) % 128, 1), 0.0)
+                value = v[f, pl.ds(8 * t, 8), :] + added
+                if f < 4 and t in ENDS_AT:
+                    own[f, ENDS_AT.index(t)] = value
+                else:
+                    v[f, pl.ds(8 * t, 8), :] = value
+        for f in range(fields):
+            for side, row in ((0, 0), (1, 15)):
+                if f < 4:
+                    rows = pl.ds(16 + row, 6, stride=16)
+                    v[f, rows, :] = v[f, rows, :] + yrecv[rnd, side, f, pl.ds(1, 6), :]
+                    at = pl.ds(7 * side, 1)
+                    for x, tile in ((0, side), (7, 2 + side)):
+                        own[f, tile, at, :] = own[f, tile, at, :] + yrecv[rnd, side, f, pl.ds(x, 1), :]
+                else:
+                    rows = pl.ds(row, 8, stride=16)
+                    v[f, rows, :] = v[f, rows, :] + yrecv[rnd, side, f]
 
     def arrive(rnd, v, x_fields):
-        for side, step in enumerate((-1, 1)):
-
-            @pl.when((gx + step >= 0) & (gx + step < n_gx))
+        for side in (0, 1):
+
+            @pl.when(beside(side))
             def _():
                 first_copy(rnd, v, side, x_fields, False).wait_recv()
+                fix_copy(rnd, side, 3 if x_fields > 3 else 2, False).wait_recv()
 
     inner = pl.ds(2, 12)
 
@@ -359,9 +397,22 @@
         return v[f, pl.ds(16, 96), :].reshape(12, 8, 128)
 
     def rims_of(rnd, v, f):
-        first = v[f, pl.ds(0, 16), :] + xrecv[rnd, 0, f]
-        last = v[f, pl.ds(112, 16), :] + xrecv[rnd, 1, f]
-        return jnp.concatenate([first.reshape(2, 8, 128), last.reshape(2, 8, 128)], axis=0)
+        lane = lax.broadcasted_iota(jnp.int32, (8, 128), 1)
+        sub = lax.broadcasted_iota(jnp.int32, (8, 128), 0)
+        last = 2 if rnd == 0 else 1
+        out = []
+        for k, t in enumerate((14, 15, 0, 1)):
+            side, half = k // 2, k % 2
+            q = 16 * (f % 3) + t
+            moved = pltpu.roll(frecv[rnd, side, f // 3], (128 - (2 * q + 1)) % 128, 1)
+            row = jnp.broadcast_to(frecv[rnd, side, last, pl.ds(2 * f + half, 1), :], (8, 128))
+            out.append(
+                own[f, k]
+                + xrecv[rnd, side, f, pl.ds(8 * half, 8), :]
+                + jnp.where((lane == 0) | (lane == 127), moved, 0.0)
+                + jnp.where(sub == 7 * half, row, 0.0)
+            )
+        return jnp.stack(out)
 
     def put_rims(ref, c, value):
         ref[c, pl.ds(0, 2)] = value[:2]
@@ -540,6 +591,7 @@
             @pl.when((gx + step >= 0) & (gx + step < n_gx))
             def _():
                 first_copy(rnd, v, side, x_fields, True).wait_send()
+                fix_copy(rnd, side, 3 if x_fields > 3 else 2, True).wait_send()
 
 
 def to_slots(field, place, out):
@@ -588,6 +640,9 @@
             pltpu.VMEM((5, 128, 128), f32),
             pltpu.VMEM((3, 128, 128), f32),
             pltpu.VMEM((3, 128, 128), f32),
+            pltpu.VMEM((4, 4, 8, 128), f32),
+            pltpu.VMEM((3, 2, 3, 8, 128), f32),
+            pltpu.VMEM((3, 2, 3, 8, 128), f32),
             pltpu.VMEM((3, 2, 5, 8, 128), f32),
             pltpu.VMEM((3, 2, 8, 128), f32),
             pltpu.VMEM((3, 2, 5, 8, 128), f32),
@@ -598,6 +653,8 @@
             pltpu.SemaphoreType.DMA((3, 2)),
             pltpu.SemaphoreType.DMA((3, 6)),
             pltpu.SemaphoreType.DMA((3, 6)),
+            pltpu.SemaphoreType.DMA((3, 2)),
+            pltpu.SemaphoreType.DMA((3, 2)),
             pltpu.SemaphoreType.DMA((3, 2)),
             pltpu.SemaphoreType.DMA((3, 2)),
         ],

time: 49 us -> 49 us (level)
  the two profiles are of different devices: /device:TPU:31 before, /device:TPU:23 now
where the time goes in v4:
time: 49 us; the launch traced here: 48.9 us
  Pallas kernels  47.6 us (97%)
  between operations  1.3 us (3%)
    pallas_call x1, Pallas kernels, shards(): pl.pallas_call(functools.partial(kernel, sizes), out_shape=(pltpu.VMEM((3...  46.6 us
    pallas_call x1, Pallas kernels, shards(): pl.pallas_call(to_slots, out_shape=jax.ShapeDtypeStruct((3, 32, 512), f32...  1 us

profile of v4, /device:TPU:23, one launch (start us, length us, event | category | flops | bytes accessed | tf_op | source)
XLA Modules:
  0.0 48.9 jit_solution(10114011933166358904)
XLA Ops:
  1.3 46.6 %solve.1 = (f32[3,128,128]{2,1,0:T(8,128)S(1)}, f32[32,32]{1,0:T(8,128)S(1)}) custom-call(f32[3,32,512]{2,1,0:T(8,128)} %bitcast.7, f32[6,16,8,128]{3,2,1,0:T(8,128)} %bitcast.6, f32[16,8,128]{2,1,0:T(8,128)} %bitcast.8, f32[1]{0:T(128)S(6)} %copy.10.low_s, f32[1]{0:T(128)S(6)} %copy.11.high_s, s32[1,32]{1,0:T(1,128)} %slot_h.1, s32[2,3,16,128]{3,2,1,0:T(8,128)} %dir_h.1, ...), custom_call_target="tpu_custom_call" | custom-call | tf_op jit(solution)/shard_map/solve/pallas_call | solution.py:618
  47.9 1.0 %to_slots.1 = f32[3,32,512]{2,1,0:T(8,128)} custom-call(f32[3,16,8,128]{3,2,1,0:T(8,128)S(1)} %bitcast.5, f32[32,32]{1,0:T(8,128)S(1)} %get-tuple-element.8.place), custom_call_target="tpu_custom_call" | custom-call | tf_op jit(solution)/shard_map/to_slots/pallas_call | solution.py:674
